TPU v7x, 32 devices: a whole 2x2x4 slice. The times are simulated.
32 devices in a mesh: leaf: 4 (over y, x), panel: 8 (over z, core).
Axes of the slice: x: 2, y: 2, z: 4, core: 2. Of those that a mesh axis runs over, the one named last changes fastest.
Arguments:
- right_sides: bfloat16 [3, 12288, 128], P(None, ('leaf', 'panel')), may hold values from -6 to 6
- inverse_low: bfloat16 [12288, 3072], P(('leaf', 'panel')), may hold values from -1 to 1, as said below
- inverse_mid: bfloat16 [12288, 6144], P(('leaf', 'panel')), may hold values from -1 to 1, as said below
- inverse_top: bfloat16 [12288, 12288], P(('leaf', 'panel')), may hold values from -1 to 1, as said below
- update_low: bfloat16 [12288, 3072], P(('leaf', 'panel')), may hold values from -0.109375 to 0.109375
- update_mid: bfloat16 [12288, 6144], P(('leaf', 'panel')), may hold values from -0.078125 to 0.078125
- slots_low: int32 [4, 3072], replicated, may hold values from 0 to 6143, as said below
- slots_mid: int32 [2, 6144], replicated, may hold values from 0 to 12287, as said below
Outputs:
- solutions: bfloat16 [3, 12288, 128], P(None, ('leaf', 'panel'))
Inputs may be any that keep to these rules, and one draw needn't show every extreme that they name: `inverse_low`: within each supernode's rows, the block is lower triangular with a unit diagonal. `inverse_mid`: within each supernode's rows, the block is lower triangular with a unit diagonal. `inverse_top`: within each supernode's rows, the block is lower triangular with a unit diagonal. `slots_low`: each row lists 3072 distinct rows of the parent supernode. `slots_mid`: each row lists 6144 distinct rows of the parent supernode.
All inputs are finite; a program needn't handle non-finite values.
Results may differ from a plain program's by a relative error of at most 0.015.
Values may be sent and summed in bfloat16 or wider, within the bound.
No kernel may reach another device: no remote copies, remote signals or barrier semaphores. Data moves between devices by JAX's collectives and lax.ppermute only.
A program may use at most 128 MiB of HBM per device.

v0:
```python
import functools
import math

import jax
import jax.numpy as jnp
from jax import lax
from jax.experimental import pallas as pl
from jax.experimental.pallas import tpu as pltpu
from jax.sharding import PartitionSpec as P


MUL = 1536
AXES = ("leaf", "panel")
CORES = 2
F32 = jnp.float32
BF16 = jnp.bfloat16


def swap_leaf(value, bit_at):
    leaves, panels = lax.axis_size("leaf"), lax.axis_size("panel")
    pairs = [
        (leaf * panels + at, (leaf ^ 1 << bit_at) * panels + at)
        for leaf in range(leaves)
        for at in range(panels)
    ]
    return lax.ppermute(value, AXES, pairs)


def swap_core(value):
    count = lax.axis_size("leaf") * lax.axis_size("panel")
    return lax.ppermute(value, AXES, [(i, i ^ 1) for i in range(count)])


def shift_depth(value, step):
    leaves, panels = lax.axis_size("leaf"), lax.axis_size("panel")
    depth = panels // CORES
    pairs = []
    for leaf in range(leaves):
        for at in range(panels):
            z, core = divmod(at, CORES)
            pairs.append((leaf * panels + at, leaf * panels + (z + step) % depth * CORES + core))
    return lax.ppermute(value, AXES, pairs)


def gather_blocks(block, bits):
    depth = lax.axis_size("panel") // CORES
    held = {(0, 0): block}
    for step in range(1, depth):
        held[0, step] = shift_depth(block, step)
    if bits >= 1:
        for step in range(depth):
            held[1, step] = swap_leaf(held[0, step], 0)
    if bits >= 2:
        for step in range(depth):
            held[2, step] = swap_leaf(held[0, step], 1)
            if step % 2:
                held[3, step] = swap_leaf(held[1, step], 1)
            else:
                held[3, step] = swap_leaf(held[2, step], 0)
    arrays = []
    for (leaf_diff, step), value in held.items():
        arrays.append((value, [(leaf_diff, step, 0)]))
        arrays.append((swap_core(value), [(leaf_diff, step, 1)]))
    return arrays


def add(*values):
    total = values[0].astype(F32)
    for value in values[1:]:
        total = total + value.astype(F32)
    return total


def scatter_groups(bits, depth):
    groups = []
    for even in reversed(range(0, depth, 2)):
        steps = [step for step in (even, even + 1) if step < depth]
        if bits == 0:
            groups.append([(0, step) for step in steps])
        elif bits == 1:
            groups.append([(1, step) for step in steps] + [(0, step) for step in steps])
        else:
            keys = [(3, even), (1, even)]
            if even + 1 < depth:
                keys += [(3, even + 1), (2, even + 1)]
            keys.append((2, even))
            if even + 1 < depth:
                keys.append((1, even + 1))
            groups.append(keys + [(0, step) for step in steps])
    return groups


def reduce_blocks(kept, sent, bits):
    depth = lax.axis_size("panel") // CORES
    groups = scatter_groups(bits, depth)
    base = {}
    for keys, mine, other in zip(groups, kept, sent):
        steps = [step for leaf_diff, step in keys if leaf_diff == 0]
        received = swap_core(other)
        part = lambda lo, hi: add(mine[lo:hi], received[lo:hi])
        first = len(keys) - len(steps)
        count = len(steps)
        if bits == 0:
            for at, step in enumerate(steps):
                base[step] = part(at, at + 1)
        elif bits == 1:
            via = swap_leaf(part(0, count).astype(BF16), 0)
            for at, step in enumerate(steps):
                base[step] = add(part(first + at, first + at + 1), via[at : at + 1])
        else:
            low = swap_leaf(part(0, 2).astype(BF16), 0)
            if count == 2:
                high = swap_leaf(part(2, 4).astype(BF16), 1)
            at = 2 * count
            next_low = swap_leaf(add(part(at, at + 1), low[:1]).astype(BF16), 1)
            base[steps[0]] = add(part(first, first + 1), low[1:2], next_low)
            if count == 2:
                next_high = swap_leaf(add(part(at + 1, at + 2), high[:1]).astype(BF16), 0)
                base[steps[1]] = add(part(first + 1, first + 2), high[1:2], next_high)
    order = [step for step in base if step]
    arrived = []
    for step in order:
        arrived.append(shift_depth(base[step].astype(BF16), step))
    return add(base[0], *arrived)[0]


def own_place(bits):
    leaf = lax.axis_index("leaf") & (2**bits - 1)
    panel = lax.axis_index("panel")
    return leaf, panel // CORES, panel % CORES


def block_index(place, depth, leaf_diff, step, swap):
    leaf, z, core = place
    return ((leaf ^ leaf_diff) * depth + lax.rem(z + step + depth, depth)) * CORES + (core ^ swap)


def widths(extent, most):
    best = 128
    for width in range(128, most + 1, 128):
        if extent % width == 0:
            best = width
    return best


def kernel_body(plan, *refs):
    mode, depth, keys_in, groups = plan["mode"], plan["depth"], plan["keys_in"], plan["groups"]
    rows, extent = plan["rows"], plan["extent"]
    load_width, mul_width = plan["load_width"], plan["mul_width"]
    refs = list(refs)
    take = lambda count: [refs.pop(0) for _ in range(count)]
    slot_ref = take(1)[0] if mode != "top" else None
    block_refs = take(len(keys_in))
    inverse_ref = take(1)[0]
    update_ref = take(1)[0] if mode != "top" else None
    prior_ref = take(1)[0] if mode == "back" else None
    solved_ref = take(1)[0] if mode == "fwd" else None
    kept_refs = take(len(groups))
    sent_refs = take(len(groups))
    inverse, update = (inverse_ref, update_ref) if plan["near"] else take(2)
    wide, narrow = take(2) if mode != "top" else (None, None)
    gathered = take(1)[0]
    result = take(1)[0] if mode != "fwd" else None
    weight_sem = None if plan["near"] else take(1)[0]
    place_in = own_place(plan["bits_in"])
    place_out = own_place(plan["bits_out"])

    def start(source, target, at):
        copies = []
        for half in range(2):
            span = pl.ds(half * (rows // 2), rows // 2)
            copy = pltpu.make_async_copy(
                source.at[span, :], target.at[span, :], weight_sem.at[2 * at + half]
            )
            copy.start()
            copies.append(copy)
        return copies

    def finish(copies):
        for copy in copies:
            copy.wait()

    update_copies, inverse_copies = [], []
    if not plan["near"]:
        if mode == "back":
            update_copies = start(update_ref, update, 0)
        inverse_copies = start(inverse_ref, inverse, 1)
        if mode == "fwd":
            update_copies = start(update_ref, update, 0)

    def span_of(place, leaf_diff, step, swap):
        index = block_index(place, depth, leaf_diff, step, swap)
        return pl.ds(pl.multiple_of(index * rows, rows), rows)

    assembled = wide if mode == "back" else gathered
    for block_ref, keys in zip(block_refs, keys_in):
        for at, (leaf_diff, step, swap) in enumerate(keys):
            block = block_ref[at * rows : (at + 1) * rows, :]
            assembled[span_of(place_in, leaf_diff, -step, swap), :] = block.astype(assembled.dtype)

    def rowwise(matrix, vector):
        total = None
        for at in range(extent // load_width):
            cols = pl.ds(at * load_width, load_width)
            term = jnp.dot(matrix[:, cols], vector[cols, :], preferred_element_type=F32)
            total = term if total is None else total + term
        return total

    def colwise(vector_t, matrix, target):
        def one(at, carry):
            span = pl.ds(pl.multiple_of(at * mul_width, mul_width), mul_width)
            product = jnp.dot(vector_t, matrix[:, span], preferred_element_type=F32)
            target[span, :] = product.astype(BF16).T.astype(target.dtype)
            return carry

        lax.fori_loop(0, extent // mul_width, one, 0)

    def over(count, chunk, body):
        def one(at, carry):
            body(pl.multiple_of(at * chunk, chunk))
            return carry

        lax.fori_loop(0, count // chunk, one, 0)

    unroll = 64
    if mode == "fwd":
        def clear(start):
            wide[pl.ds(start, 1024), :] = jnp.zeros((1024, wide.shape[1]), F32)

        over(2 * extent, 1024, clear)
    if mode == "back":
        def pick(start):
            for offset in range(unroll):
                slot = slot_ref[start + offset]
                narrow[pl.ds(start + offset, 1), :] = wide[pl.ds(slot, 1), :]

        over(extent, unroll, pick)

        def cast(start):
            gathered[pl.ds(start, 1024), :] = narrow[pl.ds(start, 1024), :].astype(BF16)

        over(extent, 1024, cast)
        finish(update_copies)
        correction = rowwise(update, gathered)
        vector = (prior_ref[...].astype(F32) - correction).astype(BF16)
    else:
        finish(inverse_copies)
        vector = rowwise(inverse, gathered).astype(BF16)
    if mode == "fwd":
        solved_ref[...] = vector
    vector_t = vector.T
    if mode == "fwd":
        finish(update_copies)
        colwise(vector_t, update, narrow)

        def spread(start):
            for offset in range(unroll):
                slot = slot_ref[start + offset]
                wide[pl.ds(slot, 1), :] = narrow[pl.ds(start + offset, 1), :]

        over(extent, unroll, spread)
        result = wide
    else:
        if mode == "back":
            finish(inverse_copies)
        colwise(vector_t, inverse, result)
    for swap, out_refs in ((1, sent_refs), (0, kept_refs)):
        for keys, out_ref in zip(groups, out_refs):
            for at, (leaf_diff, step) in enumerate(keys):
                out_ref[at] = result[span_of(place_out, leaf_diff, step, swap), :].astype(BF16)


def load_kernel(count, *refs):
    sources, targets, sem = refs[:count], refs[count + 1 : 2 * count + 1], refs[-1]
    copies = []
    for at, (source, target) in enumerate(zip(sources, targets)):
        rows = source.shape[0] // 2
        for half in range(2):
            span = pl.ds(half * rows, rows)
            copy = pltpu.make_async_copy(
                source.at[span, :], target.at[span, :], sem.at[2 * at + half]
            )
            copy.start()
            copies.append(copy)
    for copy in copies:
        copy.wait()


def load(matrices, after):
    hbm_spec = pl.BlockSpec(memory_space=pltpu.MemorySpace.HBM)
    vmem_spec = pl.BlockSpec(memory_space=pltpu.VMEM)
    count = len(matrices)
    size = sum(math.prod(m.shape) * m.dtype.itemsize for m in matrices)
    out_shape = [jax.ShapeDtypeStruct(m.shape, m.dtype) for m in matrices]
    matrices = [pltpu.with_memory_space_constraint(m, pltpu.MemorySpace.HBM) for m in matrices]
    return pl.pallas_call(
        functools.partial(load_kernel, count),
        out_shape=out_shape,
        in_specs=[hbm_spec] * count + [pl.BlockSpec(memory_space=pl.ANY)],
        out_specs=[vmem_spec] * count,
        scratch_shapes=[pltpu.SemaphoreType.DMA((2 * count,))],
        compiler_params=pltpu.CompilerParams(vmem_limit_bytes=4 * 2**20),
        cost_estimate=pl.CostEstimate(flops=0, bytes_accessed=2 * size, transcendentals=0),
    )(*matrices, after)


def run_level(mode, level, blocks, inverse, update=None, slots=None, prior=None, near=False):
    rows, extent = inverse.shape
    depth = lax.axis_size("panel") // CORES
    vec = blocks[0][0].shape[1]
    bits_in = {"fwd": level, "top": level, "back": level + 1}[mode]
    bits_out = {"fwd": level + 1, "top": level, "back": level}[mode]
    keys_in = [keys for _, keys in blocks]
    groups = scatter_groups(bits_out, depth)
    load_width = widths(extent, 3072)
    plan = dict(
        near=near,
        bits_in=bits_in, bits_out=bits_out, depth=depth, mode=mode, keys_in=keys_in,
        groups=groups, rows=rows, extent=extent, load_width=load_width, mul_width=widths(extent, MUL),
    )
    vmem_spec = pl.BlockSpec(memory_space=pltpu.VMEM)
    operands, in_specs = [], []
    if mode != "top":
        operands.append(slots)
        in_specs.append(pl.BlockSpec(memory_space=pltpu.SMEM))
    for value, _ in blocks:
        operands.append(value)
        in_specs.append(vmem_spec)
    far_spec = pl.BlockSpec(memory_space=pltpu.MemorySpace.HBM)
    far = lambda value: pltpu.with_memory_space_constraint(value, pltpu.MemorySpace.HBM)
    for weights in (inverse, update):
        if weights is not None:
            operands.append(weights if near else far(weights))
            in_specs.append(vmem_spec if near else far_spec)
    if mode == "back":
        operands.append(prior)
        in_specs.append(vmem_spec)
    out_shape = []
    if mode == "fwd":
        out_shape.append(jax.ShapeDtypeStruct((rows, vec), BF16))
    for keys in groups * 2:
        out_shape.append(jax.ShapeDtypeStruct((len(keys), rows, vec), BF16))
    scratch = [] if near else [pltpu.VMEM((rows, extent), BF16)] * 2
    if mode != "top":
        scratch += [pltpu.VMEM((2 * extent, vec), F32), pltpu.VMEM((extent, vec), F32)]
    scratch.append(pltpu.VMEM((extent, vec), BF16))
    if mode != "fwd":
        scratch.append(pltpu.VMEM((extent, vec), BF16))
    held = sum(math.prod(ref.shape) * ref.dtype.itemsize for ref in scratch)
    if not near:
        scratch.append(pltpu.SemaphoreType.DMA((4,)))
    outs = pl.pallas_call(
        functools.partial(kernel_body, plan),
        out_shape=out_shape,
        in_specs=in_specs,
        out_specs=[vmem_spec] * len(out_shape),
        scratch_shapes=scratch,
        compiler_params=pltpu.CompilerParams(vmem_limit_bytes=held + 12 * 2**20),
    )(*operands)
    outs = list(outs)
    solved = outs.pop(0) if mode == "fwd" else None
    return solved, outs[: len(groups)], outs[len(groups) :]


def on_device(
    right_sides, inverse_low, inverse_mid, inverse_top, update_low, update_mid, slots_low, slots_mid
):
    inverses = (inverse_low, inverse_mid, inverse_top)
    updates = (update_low, update_mid)
    lists = (slots_low, slots_mid)
    height = len(inverses)
    leaf_at = lax.axis_index("leaf")
    slot_rows = [
        lax.dynamic_index_in_dim(lists[level], leaf_at >> level, 0, keepdims=False)
        for level in range(height - 1)
    ]
    solved = []
    local_rows = right_sides[0]
    for level in range(height - 1):
        inverse, update = inverses[level], updates[level]
        if level == 0:
            inverse, update = load((inverse, update), local_rows)
        blocks = gather_blocks(local_rows, level)
        done, kept, sent = run_level(
            "fwd", level, blocks, inverse, update, slot_rows[level], near=level == 0
        )
        solved.append(done)
        carried = reduce_blocks(kept, sent, level + 1)
        local_rows = (right_sides[level + 1].astype(F32) - carried).astype(BF16)
    top = height - 1
    (inverse,) = load((inverses[top],), local_rows)
    blocks = gather_blocks(local_rows, top)
    _, kept, sent = run_level("top", top, blocks, inverse, near=True)
    results = [None] * height
    results[top] = reduce_blocks(kept, sent, top).astype(BF16)
    for level in reversed(range(top)):
        inverse, update = load((inverses[level], updates[level]), results[level + 1])
        blocks = gather_blocks(results[level + 1], level + 1)
        _, kept, sent = run_level(
            "back", level, blocks, inverse, update, slot_rows[level], solved[level], near=True
        )
        results[level] = reduce_blocks(kept, sent, level).astype(BF16)
    return jnp.stack(results)


def solution(mesh):
    both = ("leaf", "panel")

    return jax.shard_map(
        on_device,
        mesh=mesh,
        in_specs=(P(None, both, None),) + (P(both, None),) * 5 + (P(), P()),
        out_specs=P(None, both, None),
        check_vma=False,
    )
```

profile of v0, /device:TPU:0, one launch (start us, length us, event | category | flops | bytes accessed | tf_op | source)
XLA Modules:
  0.0 292.8 jit_solution(18217838480738223435)
XLA Ops:
  0.9 5.1 %collective-permute-start.5 = (bf16[384,128]{1,0:T(8,128)(2,1)S(1)}, bf16[384,128]{1,0:T(8,128)(2,1)S(1)}, u32[]{:S(2)}, u32[]{:S(2)}) collective-permute-start(bf16[384,128]{1,0:T(8,128)(2,1)S(1)} %slice_bitcast_fusion.refs_2_.refs_1_), channel_id=1, source_target_pairs={{0,6},{1,7},{2,0},{3,1},{4,2},{5,3},{6,4},{7,5},{8,14},{9,15},{10,... | collective-permute-start | bytes 294920 | tf_op jit(solution)/shard_map/ppermute | solution.py:42
  7.0 2.2 collective-permute-done.5.refs_7_
  9.2 5.6 %collective-permute-done.3.refs_5_ = bf16[384,128]{1,0:T(8,128)(2,1)S(1)} collective-permute-done((bf16[384,128]{1,0:T(8,128)(2,1)S(1)}, bf16[384,128]{1,0:T(8,128)(2,1)S(1)}, u32[]{:S(2)}, u32[]{:S(2)}) %collective-permute-start.3) | collective-permute-done | bytes 98336 | tf_op jit(solution)/shard_map/ppermute | solution.py:42
  16.1 2.4 shard_map.82
  18.5 5.5 %shard_map.83 = (bf16[384,128]{1,0:T(8,128)(2,1)S(1)}, bf16[4,384,128]{2,1,0:T(8,128)(2,1)S(1)}, bf16[4,384,128]{2,1,0:T(8,128)(2,1)S(1)}, bf16[4,384,128]{2,1,0:T(8,128)(2,1)S(1)}, bf16[4,384,128]{2,1,0:T(8,128)(2,1)S(1)}) custom-call(s32[3072]{0:T(1024)S(1)} %bitcast.27, bf16[384,128]{1,0:T(8,128)(2,1)S(1)} %slice_bitcast_fusion.refs_2_.refs_1_, ...), custom_call_target="tpu_custom_call" | custom-call | tf_op jit(solution)/shard_map/pallas_call | solution.py:352
  28.1 5.6 %collective-permute-done.8 = bf16[2,384,128]{2,1,0:T(8,128)(2,1)S(1)} collective-permute-done((bf16[2,384,128]{2,1,0:T(8,128)(2,1)S(1)}, bf16[2,384,128]{2,1,0:T(8,128)(2,1)S(1)}, u32[]{:S(2)}, u32[]{:S(2)}) %collective-permute-start.8) | collective-permute-done | bytes 196640 | tf_op jit(solution)/shard_map/ppermute | solution.py:26
  33.8 3.3 %collective-permute-done.10 = bf16[2,384,128]{2,1,0:T(8,128)(2,1)S(1)} collective-permute-done((bf16[2,384,128]{2,1,0:T(8,128)(2,1)S(1)}, bf16[2,384,128]{2,1,0:T(8,128)(2,1)S(1)}, u32[]{:S(2)}, u32[]{:S(2)}) %collective-permute-start.10) | collective-permute-done | bytes 196640 | tf_op jit(solution)/shard_map/ppermute | solution.py:26
  37.2 2.2 collective-permute-start.11
  40.6 4.1 %collective-permute-done.11 = bf16[1,384,128]{2,1,0:T(8,128)(2,1)S(1)} collective-permute-done((bf16[1,384,128]{2,1,0:T(8,128)(2,1)S(1)}, bf16[1,384,128]{2,1,0:T(8,128)(2,1)S(1)}, u32[]{:S(2)}, u32[]{:S(2)}) %collective-permute-start.11) | collective-permute-done | bytes 98336 | tf_op jit(solution)/shard_map/ppermute | solution.py:42
  47.0 3.2 %collective-permute-start.19 = (bf16[384,128]{1,0:T(8,128)(2,1)S(1)}, bf16[384,128]{1,0:T(8,128)(2,1)S(1)}, u32[]{:S(2)}, u32[]{:S(2)}) collective-permute-start(bf16[384,128]{1,0:T(8,128)(2,1)S(1)} %fusion.refs_1_), channel_id=1, source_target_pairs={{0,6},{1,7},{2,0},{3,1},{4,2},{5,3},{6,4},{7,5},{8,14},{9,15},{10,... | collective-permute-start | bytes 294920 | tf_op jit(solution)/shard_map/ppermute | solution.py:42
  53.4 5.4 %collective-permute-done.17.refs_5_ = bf16[384,128]{1,0:T(8,128)(2,1)S(1)} collective-permute-done((bf16[384,128]{1,0:T(8,128)(2,1)S(1)}, bf16[384,128]{1,0:T(8,128)(2,1)S(1)}, u32[]{:S(2)}, u32[]{:S(2)}) %collective-permute-start.17) | collective-permute-done | bytes 98336 | tf_op jit(solution)/shard_map/ppermute | solution.py:42
  61.4 3.0 %collective-permute-done.25.refs_13_ = bf16[384,128]{1,0:T(8,128)(2,1)S(1)} collective-permute-done((bf16[384,128]{1,0:T(8,128)(2,1)S(1)}, bf16[384,128]{1,0:T(8,128)(2,1)S(1)}, u32[]{:S(2)}, u32[]{:S(2)}) %collective-permute-start.25) | collective-permute-done | bytes 98336 | tf_op jit(solution)/shard_map/ppermute | solution.py:26
  67.4 12.2 %shard_map.84 = (bf16[384,128]{1,0:T(8,128)(2,1)S(1)}, bf16[8,384,128]{2,1,0:T(8,128)(2,1)S(1)}, bf16[8,384,128]{2,1,0:T(8,128)(2,1)S(1)}, bf16[8,384,128]{2,1,0:T(8,128)(2,1)S(1)}, bf16[8,384,128]{2,1,0:T(8,128)(2,1)S(1)}) custom-call(s32[6144]{0:T(1024)S(1)} %bitcast.25, bf16[384,128]{1,0:T(8,128)(2,1)S(1)} %fusion.refs_1_, ...), custom_call_target="tpu_custom_call" | custom-call | tf_op jit(solution)/shard_map/pallas_call | solution.py:352
  86.4 3.5 %collective-permute-done.33 = bf16[2,384,128]{2,1,0:T(8,128)(2,1)S(1)} collective-permute-done((bf16[2,384,128]{2,1,0:T(8,128)(2,1)S(1)}, bf16[2,384,128]{2,1,0:T(8,128)(2,1)S(1)}, u32[]{:S(2)}, u32[]{:S(2)}) %collective-permute-start.33) | collective-permute-done | bytes 196640 | tf_op jit(solution)/shard_map/ppermute | solution.py:26
  96.4 1.8 collective-permute-done.34
  104.7 2.6 collective-permute-done.41
  107.4 2.1 collective-permute-done.35
  117.9 3.2 %collective-permute-done.45.refs_4_ = bf16[384,128]{1,0:T(8,128)(2,1)S(1)} collective-permute-done((bf16[384,128]{1,0:T(8,128)(2,1)S(1)}, bf16[384,128]{1,0:T(8,128)(2,1)S(1)}, u32[]{:S(2)}, u32[]{:S(2)}) %collective-permute-start.45) | collective-permute-done | bytes 98336 | tf_op jit(solution)/shard_map/ppermute | solution.py:42
  128.0 2.2 collective-permute-start.51
  132.9 2.0 collective-permute-start.67
  138.9 2.4 collective-permute-done.63.refs_22_
  141.3 3.8 %shard_map.85.refs_32_ = bf16[384,12288]{1,0:T(8,128)(2,1)S(1)} custom-call(bf16[384,12288]{1,0:T(8,128)(2,1)} %refs_0_.5, bf16[384,128]{1,0:T(8,128)(2,1)S(1)} %fusion.1.refs_1_.refs_0_), custom_call_target="tpu_custom_call" | custom-call | bytes 18874368 | tf_op jit(solution)/shard_map/pallas_call | solution.py:296
  145.1 7.0 %shard_map.86 = (bf16[8,384,128]{2,1,0:T(8,128)(2,1)S(1)}, bf16[8,384,128]{2,1,0:T(8,128)(2,1)S(1)}, bf16[8,384,128]{2,1,0:T(8,128)(2,1)S(1)}, bf16[8,384,128]{2,1,0:T(8,128)(2,1)S(1)}) custom-call(bf16[384,128]{1,0:T(8,128)(2,1)S(1)} %fusion.1.refs_1_.refs_0_, bf16[384,128]{1,0:T(8,128)(2,1)S(1)} %collective-permute-done.42.refs_1_, ...), custom_call_target="tpu_custom_call" | custom-call | tf_op jit(solution)/shard_map/pallas_call | solution.py:352
  152.8 1.8 collective-permute-done.76
  159.6 3.0 %collective-permute-done.77 = bf16[2,384,128]{2,1,0:T(8,128)(2,1)S(1)} collective-permute-done((bf16[2,384,128]{2,1,0:T(8,128)(2,1)S(1)}, bf16[2,384,128]{2,1,0:T(8,128)(2,1)S(1)}, u32[]{:S(2)}, u32[]{:S(2)}) %collective-permute-start.77) | collective-permute-done | bytes 196640 | tf_op jit(solution)/shard_map/ppermute | solution.py:26
  163.6 2.6 collective-permute-done.74
  169.6 2.1 collective-permute-done.78
  173.0 1.8 collective-permute-start.79
  179.5 2.3 collective-permute-done.79
  184.2 2.5 collective-permute-start.91
  189.1 6.0 %collective-permute-done.89.refs_5_ = bf16[384,128]{1,0:T(8,128)(2,1)S(1)} collective-permute-done((bf16[384,128]{1,0:T(8,128)(2,1)S(1)}, bf16[384,128]{1,0:T(8,128)(2,1)S(1)}, u32[]{:S(2)}, u32[]{:S(2)}) %collective-permute-start.89) | collective-permute-done | bytes 98336 | tf_op jit(solution)/shard_map/ppermute | solution.py:42
  203.7 2.7 collective-permute-done.105.refs_21_
  208.1 3.0 %collective-permute-done.115.refs_31_ = bf16[384,128]{1,0:T(8,128)(2,1)S(1)} collective-permute-done((bf16[384,128]{1,0:T(8,128)(2,1)S(1)}, bf16[384,128]{1,0:T(8,128)(2,1)S(1)}, u32[]{:S(2)}, u32[]{:S(2)}) %collective-permute-start.115) | collective-permute-done | bytes 98336 | tf_op jit(solution)/shard_map/ppermute | solution.py:26
  213.2 2.5 collective-permute-done.107.refs_23_
  215.6 3.8 %shard_map.87 = (bf16[384,6144]{1,0:T(8,128)(2,1)S(1)}, bf16[384,6144]{1,0:T(8,128)(2,1)S(1)}) custom-call(bf16[384,6144]{1,0:T(8,128)(2,1)} %refs_0_.6, bf16[384,6144]{1,0:T(8,128)(2,1)} %refs_1_.4, bf16[384,128]{1,0:T(8,128)(2,1)S(1)} %bitcast.16), custom_call_target="tpu_custom_call" | custom-call | bytes 18874368 | tf_op jit(solution)/shard_map/pallas_call | solution.py:296
  219.5 10.4 %shard_map.88 = (bf16[4,384,128]{2,1,0:T(8,128)(2,1)S(1)}, bf16[4,384,128]{2,1,0:T(8,128)(2,1)S(1)}, bf16[4,384,128]{2,1,0:T(8,128)(2,1)S(1)}, bf16[4,384,128]{2,1,0:T(8,128)(2,1)S(1)}) custom-call(s32[6144]{0:T(1024)S(1)} %bitcast.26, bf16[384,128]{1,0:T(8,128)(2,1)S(1)} %bitcast.17, bf16[384,128]{1,0:T(8,128)(2,1)S(1)} %collective-permute-done.86.refs_2_, ...), custom_call_target="tpu_custom_call" | custom-call | tf_op jit(solution)/shard_map/pallas_call | solution.py:352
  234.1 5.6 %collective-permute-done.118 = bf16[2,384,128]{2,1,0:T(8,128)(2,1)S(1)} collective-permute-done((bf16[2,384,128]{2,1,0:T(8,128)(2,1)S(1)}, bf16[2,384,128]{2,1,0:T(8,128)(2,1)S(1)}, u32[]{:S(2)}, u32[]{:S(2)}) %collective-permute-start.118) | collective-permute-done | bytes 196640 | tf_op jit(solution)/shard_map/ppermute | solution.py:26
  239.9 3.5 %collective-permute-done.120 = bf16[2,384,128]{2,1,0:T(8,128)(2,1)S(1)} collective-permute-done((bf16[2,384,128]{2,1,0:T(8,128)(2,1)S(1)}, bf16[2,384,128]{2,1,0:T(8,128)(2,1)S(1)}, u32[]{:S(2)}, u32[]{:S(2)}) %collective-permute-start.120) | collective-permute-done | bytes 196640 | tf_op jit(solution)/shard_map/ppermute | solution.py:26
  247.1 3.5 %collective-permute-done.121 = bf16[1,384,128]{2,1,0:T(8,128)(2,1)S(1)} collective-permute-done((bf16[1,384,128]{2,1,0:T(8,128)(2,1)S(1)}, bf16[1,384,128]{2,1,0:T(8,128)(2,1)S(1)}, u32[]{:S(2)}, u32[]{:S(2)}) %collective-permute-start.121) | collective-permute-done | bytes 98336 | tf_op jit(solution)/shard_map/ppermute | solution.py:42
  251.1 3.2 %collective-permute-start.129 = (bf16[384,128]{1,0:T(8,128)(2,1)S(1)}, bf16[384,128]{1,0:T(8,128)(2,1)S(1)}, u32[]{:S(2)}, u32[]{:S(2)}) collective-permute-start(bf16[384,128]{1,0:T(8,128)(2,1)S(1)} %bitcast.19), channel_id=1, source_target_pairs={{0,6},{1,7},{2,0},{3,1},{4,2},{5,3},{6,4},{7,5},{8,14},{9,15},{10,... | collective-permute-start | bytes 294920 | tf_op jit(solution)/shard_map/ppermute | solution.py:42
  255.4 2.0 collective-permute-done.129.refs_7_
  258.9 4.9 %collective-permute-done.127.refs_5_ = bf16[384,128]{1,0:T(8,128)(2,1)S(1)} collective-permute-done((bf16[384,128]{1,0:T(8,128)(2,1)S(1)}, bf16[384,128]{1,0:T(8,128)(2,1)S(1)}, u32[]{:S(2)}, u32[]{:S(2)}) %collective-permute-start.127) | collective-permute-done | bytes 98336 | tf_op jit(solution)/shard_map/ppermute | solution.py:42
  266.4 3.0 %collective-permute-done.135.refs_13_ = bf16[384,128]{1,0:T(8,128)(2,1)S(1)} collective-permute-done((bf16[384,128]{1,0:T(8,128)(2,1)S(1)}, bf16[384,128]{1,0:T(8,128)(2,1)S(1)}, u32[]{:S(2)}, u32[]{:S(2)}) %collective-permute-start.135) | collective-permute-done | bytes 98336 | tf_op jit(solution)/shard_map/ppermute | solution.py:26
  271.1 2.4 shard_map.89
  273.6 5.5 %shard_map.90 = (bf16[2,384,128]{2,1,0:T(8,128)(2,1)S(1)}, bf16[2,384,128]{2,1,0:T(8,128)(2,1)S(1)}, bf16[2,384,128]{2,1,0:T(8,128)(2,1)S(1)}, bf16[2,384,128]{2,1,0:T(8,128)(2,1)S(1)}) custom-call(s32[3072]{0:T(1024)S(1)} %bitcast.28, bf16[384,128]{1,0:T(8,128)(2,1)S(1)} %bitcast.24, bf16[384,128]{1,0:T(8,128)(2,1)S(1)} %collective-permute-done.124.refs_2_, ...), custom_call_target="tpu_custom_call" | custom-call | tf_op jit(solution)/shard_map/pallas_call | solution.py:352
  282.2 2.7 collective-permute-start.142
  284.8 3.5 %collective-permute-done.143 = bf16[1,384,128]{2,1,0:T(8,128)(2,1)S(1)} collective-permute-done((bf16[1,384,128]{2,1,0:T(8,128)(2,1)S(1)}, bf16[1,384,128]{2,1,0:T(8,128)(2,1)S(1)}, u32[]{:S(2)}, u32[]{:S(2)}) %collective-permute-start.143) | collective-permute-done | bytes 98336 | tf_op jit(solution)/shard_map/ppermute | solution.py:42
  288.4 3.6 %collective-permute-done.141 = bf16[1,384,128]{2,1,0:T(8,128)(2,1)S(1)} collective-permute-done((bf16[1,384,128]{2,1,0:T(8,128)(2,1)S(1)}, bf16[1,384,128]{2,1,0:T(8,128)(2,1)S(1)}, u32[]{:S(2)}, u32[]{:S(2)}) %collective-permute-start.141) | collective-permute-done | bytes 98336 | tf_op jit(solution)/shard_map/ppermute | solution.py:42
  (288 shorter events, 113.8 us)
Async XLA Ops:
  0.9 8.3 %collective-permute-start.5 = (bf16[384,128]{1,0:T(8,128)(2,1)S(1)}, bf16[384,128]{1,0:T(8,128)(2,1)S(1)}, u32[]{:S(2)}, u32[]{:S(2)}) collective-permute-start(bf16[384,128]{1,0:T(8,128)(2,1)S(1)} %slice_bitcast_fusion.refs_2_.refs_1_), channel_id=1, source_target_pairs={{0,6},{1,7},{2,0},{3,1},{4,2},{5,3},{6,4},{7,5},{8,14},{9,15},{10,... | collective-permute-start | bytes 294920 | tf_op jit(solution)/shard_map/ppermute | solution.py:42
  6.0 8.8 %collective-permute-start.3 = (bf16[384,128]{1,0:T(8,128)(2,1)S(1)}, bf16[384,128]{1,0:T(8,128)(2,1)S(1)}, u32[]{:S(2)}, u32[]{:S(2)}) collective-permute-start(bf16[384,128]{1,0:T(8,128)(2,1)S(1)} %slice_bitcast_fusion.refs_2_.refs_1_), channel_id=1, source_target_pairs={{0,4},{1,5},{2,6},{3,7},{4,0},{5,1},{6,2},{7,3},{8,12},{9,13},{10,... | collective-permute-start | bytes 294920 | tf_op jit(solution)/shard_map/ppermute | solution.py:42
  6.0 8.8 %collective-permute-start.1 = (bf16[384,128]{1,0:T(8,128)(2,1)S(1)}, bf16[384,128]{1,0:T(8,128)(2,1)S(1)}, u32[]{:S(2)}, u32[]{:S(2)}) collective-permute-start(bf16[384,128]{1,0:T(8,128)(2,1)S(1)} %slice_bitcast_fusion.refs_2_.refs_1_), channel_id=1, source_target_pairs={{0,2},{1,3},{2,4},{3,5},{4,6},{5,7},{6,0},{7,1},{8,10},{9,11},{10,... | collective-permute-start | bytes 294920 | tf_op jit(solution)/shard_map/ppermute | solution.py:42
  7.0 11.5 %collective-permute-start = (bf16[384,128]{1,0:T(8,128)(2,1)S(1)}, bf16[384,128]{1,0:T(8,128)(2,1)S(1)}, u32[]{:S(2)}, u32[]{:S(2)}) collective-permute-start(bf16[384,128]{1,0:T(8,128)(2,1)S(1)} %slice_bitcast_fusion.refs_2_.refs_1_), channel_id=1, source_target_pairs={{0,1},{1,0},{2,3},{3,2},{4,5},{5,4},{6,7},{7,6},{8,9},{9,8},{10,11... | collective-permute-start | bytes 294920 | tf_op jit(solution)/shard_map/ppermute | solution.py:31
  9.2 9.3 %collective-permute-start.6 = (bf16[384,128]{1,0:T(8,128)(2,1)S(1)}, bf16[384,128]{1,0:T(8,128)(2,1)S(1)}, u32[]{:S(2)}, u32[]{:S(2)}) collective-permute-start(bf16[384,128]{1,0:T(8,128)(2,1)S(1)} %collective-permute-done.5.refs_7_), channel_id=1, source_target_pairs={{0,1},{1,0},{2,3},{3,2},{4,5},{5,4},{6,7},{7,6},{8,9},{9,8},{10,11... | collective-permute-start | bytes 294920 | tf_op jit(solution)/shard_map/ppermute | solution.py:31
  25.9 7.8 %collective-permute-start.8 = (bf16[2,384,128]{2,1,0:T(8,128)(2,1)S(1)}, bf16[2,384,128]{2,1,0:T(8,128)(2,1)S(1)}, u32[]{:S(2)}, u32[]{:S(2)}) collective-permute-start(bf16[2,384,128]{2,1,0:T(8,128)(2,1)S(1)} %add_convert_fusion.11), channel_id=1, source_target_pairs={{0,8},{1,9},{2,10},{3,11},{4,12},{5,13},{6,14},{7,15},{8,0},{9,1},... | collective-permute-start | bytes 589832 | tf_op jit(solution)/shard_map/ppermute | solution.py:26
  27.5 9.6 %collective-permute-start.10 = (bf16[2,384,128]{2,1,0:T(8,128)(2,1)S(1)}, bf16[2,384,128]{2,1,0:T(8,128)(2,1)S(1)}, u32[]{:S(2)}, u32[]{:S(2)}) collective-permute-start(bf16[2,384,128]{2,1,0:T(8,128)(2,1)S(1)} %add_convert_fusion.10), channel_id=1, source_target_pairs={{0,8},{1,9},{2,10},{3,11},{4,12},{5,13},{6,14},{7,15},{8,0},{9,1},... | collective-permute-start | bytes 589832 | tf_op jit(solution)/shard_map/ppermute | solution.py:26
  37.2 7.5 %collective-permute-start.11 = (bf16[1,384,128]{2,1,0:T(8,128)(2,1)S(1)}, bf16[1,384,128]{2,1,0:T(8,128)(2,1)S(1)}, u32[]{:S(2)}, u32[]{:S(2)}) collective-permute-start(bf16[1,384,128]{2,1,0:T(8,128)(2,1)S(1)} %get-tuple-element.79), channel_id=1, source_target_pairs={{0,4},{1,5},{2,6},{3,7},{4,0},{5,1},{6,2},{7,3},{8,12},{9,13},{10,... | collective-permute-start | bytes 294920 | tf_op jit(solution)/shard_map/ppermute | solution.py:42
  50.2 8.6 %collective-permute-start.17 = (bf16[384,128]{1,0:T(8,128)(2,1)S(1)}, bf16[384,128]{1,0:T(8,128)(2,1)S(1)}, u32[]{:S(2)}, u32[]{:S(2)}) collective-permute-start(bf16[384,128]{1,0:T(8,128)(2,1)S(1)} %fusion.refs_1_), channel_id=1, source_target_pairs={{0,4},{1,5},{2,6},{3,7},{4,0},{5,1},{6,2},{7,3},{8,12},{9,13},{10,... | collective-permute-start | bytes 294920 | tf_op jit(solution)/shard_map/ppermute | solution.py:42
  50.2 8.6 %collective-permute-start.15 = (bf16[384,128]{1,0:T(8,128)(2,1)S(1)}, bf16[384,128]{1,0:T(8,128)(2,1)S(1)}, u32[]{:S(2)}, u32[]{:S(2)}) collective-permute-start(bf16[384,128]{1,0:T(8,128)(2,1)S(1)} %fusion.refs_1_), channel_id=1, source_target_pairs={{0,2},{1,3},{2,4},{3,5},{4,6},{5,7},{6,0},{7,1},{8,10},{9,11},{10,... | collective-permute-start | bytes 294920 | tf_op jit(solution)/shard_map/ppermute | solution.py:42
  50.8 8.6 %collective-permute-start.14 = (bf16[384,128]{1,0:T(8,128)(2,1)S(1)}, bf16[384,128]{1,0:T(8,128)(2,1)S(1)}, u32[]{:S(2)}, u32[]{:S(2)}) collective-permute-start(bf16[384,128]{1,0:T(8,128)(2,1)S(1)} %fusion.refs_1_), channel_id=1, source_target_pairs={{0,1},{1,0},{2,3},{3,2},{4,5},{5,4},{6,7},{7,6},{8,9},{9,8},{10,11... | collective-permute-start | bytes 294920 | tf_op jit(solution)/shard_map/ppermute | solution.py:31
  50.8 10.1 %collective-permute-start.22 = (bf16[384,128]{1,0:T(8,128)(2,1)S(1)}, bf16[384,128]{1,0:T(8,128)(2,1)S(1)}, u32[]{:S(2)}, u32[]{:S(2)}) collective-permute-start(bf16[384,128]{1,0:T(8,128)(2,1)S(1)} %collective-permute-done.21.refs_9_), channel_id=1, source_target_pairs={{0,1},{1,0},{2,3},{3,2},{4,5},{5,4},{6,7},{7,6},{8,9},{9,8},{10,11... | collective-permute-start | bytes 294920 | tf_op jit(solution)/shard_map/ppermute | solution.py:31
  52.9 8.0 %collective-permute-start.27 = (bf16[384,128]{1,0:T(8,128)(2,1)S(1)}, bf16[384,128]{1,0:T(8,128)(2,1)S(1)}, u32[]{:S(2)}, u32[]{:S(2)}) collective-permute-start(bf16[384,128]{1,0:T(8,128)(2,1)S(1)} %collective-permute-done.19.refs_7_), channel_id=1, source_target_pairs={{0,8},{1,9},{2,10},{3,11},{4,12},{5,13},{6,14},{7,15},{8,0},{9,1},... | collective-permute-start | bytes 294920 | tf_op jit(solution)/shard_map/ppermute | solution.py:26
  82.1 7.8 %collective-permute-start.33 = (bf16[2,384,128]{2,1,0:T(8,128)(2,1)S(1)}, bf16[2,384,128]{2,1,0:T(8,128)(2,1)S(1)}, u32[]{:S(2)}, u32[]{:S(2)}) collective-permute-start(bf16[2,384,128]{2,1,0:T(8,128)(2,1)S(1)} %get-tuple-element.75), channel_id=1, source_target_pairs={{0,8},{1,9},{2,10},{3,11},{4,12},{5,13},{6,14},{7,15},{8,0},{9,1},... | collective-permute-start | bytes 589832 | tf_op jit(solution)/shard_map/ppermute | solution.py:26
  83.2 10.1 %collective-permute-start.30 = (bf16[2,384,128]{2,1,0:T(8,128)(2,1)S(1)}, bf16[2,384,128]{2,1,0:T(8,128)(2,1)S(1)}, u32[]{:S(2)}, u32[]{:S(2)}) collective-permute-start(bf16[2,384,128]{2,1,0:T(8,128)(2,1)S(1)} %get-tuple-element.71), channel_id=1, source_target_pairs={{0,8},{1,9},{2,10},{3,11},{4,12},{5,13},{6,14},{7,15},{8,0},{9,1},... | collective-permute-start | bytes 589832 | tf_op jit(solution)/shard_map/ppermute | solution.py:26
  84.4 9.0 %collective-permute-start.39 = (bf16[2,384,128]{2,1,0:T(8,128)(2,1)S(1)}, bf16[2,384,128]{2,1,0:T(8,128)(2,1)S(1)}, u32[]{:S(2)}, u32[]{:S(2)}) collective-permute-start(bf16[2,384,128]{2,1,0:T(8,128)(2,1)S(1)} %get-tuple-element.72), channel_id=1, source_target_pairs={{0,16},{1,17},{2,18},{3,19},{4,20},{5,21},{6,22},{7,23},{8,24},{9,... | collective-permute-start | bytes 589832 | tf_op jit(solution)/shard_map/ppermute | solution.py:26
  85.9 10.5 %collective-permute-start.36 = (bf16[2,384,128]{2,1,0:T(8,128)(2,1)S(1)}, bf16[2,384,128]{2,1,0:T(8,128)(2,1)S(1)}, u32[]{:S(2)}, u32[]{:S(2)}) collective-permute-start(bf16[2,384,128]{2,1,0:T(8,128)(2,1)S(1)} %get-tuple-element.76), channel_id=1, source_target_pairs={{0,16},{1,17},{2,18},{3,19},{4,20},{5,21},{6,22},{7,23},{8,24},{9,... | collective-permute-start | bytes 589832 | tf_op jit(solution)/shard_map/ppermute | solution.py:26
  90.0 8.2 %collective-permute-start.34 = (bf16[1,384,128]{2,1,0:T(8,128)(2,1)S(1)}, bf16[1,384,128]{2,1,0:T(8,128)(2,1)S(1)}, u32[]{:S(2)}, u32[]{:S(2)}) collective-permute-start(bf16[1,384,128]{2,1,0:T(8,128)(2,1)S(1)} %add_convert_fusion.33), channel_id=1, source_target_pairs={{0,16},{1,17},{2,18},{3,19},{4,20},{5,21},{6,22},{7,23},{8,24},{9,... | collective-permute-start | bytes 294920 | tf_op jit(solution)/shard_map/ppermute | solution.py:26
  93.4 11.3 %collective-permute-start.31 = (bf16[1,384,128]{2,1,0:T(8,128)(2,1)S(1)}, bf16[1,384,128]{2,1,0:T(8,128)(2,1)S(1)}, u32[]{:S(2)}, u32[]{:S(2)}) collective-permute-start(bf16[1,384,128]{2,1,0:T(8,128)(2,1)S(1)} %get-tuple-element.69), channel_id=1, source_target_pairs={{0,16},{1,17},{2,18},{3,19},{4,20},{5,21},{6,22},{7,23},{8,24},{9,... | collective-permute-start | bytes 294920 | tf_op jit(solution)/shard_map/ppermute | solution.py:26
  101.8 7.7 %collective-permute-start.35 = (bf16[1,384,128]{2,1,0:T(8,128)(2,1)S(1)}, bf16[1,384,128]{2,1,0:T(8,128)(2,1)S(1)}, u32[]{:S(2)}, u32[]{:S(2)}) collective-permute-start(bf16[1,384,128]{2,1,0:T(8,128)(2,1)S(1)} %get-tuple-element.73), channel_id=1, source_target_pairs={{0,4},{1,5},{2,6},{3,7},{4,0},{5,1},{6,2},{7,3},{8,12},{9,13},{10,... | collective-permute-start | bytes 294920 | tf_op jit(solution)/shard_map/ppermute | solution.py:42
  113.3 7.7 %collective-permute-start.45 = (bf16[384,128]{1,0:T(8,128)(2,1)S(1)}, bf16[384,128]{1,0:T(8,128)(2,1)S(1)}, u32[]{:S(2)}, u32[]{:S(2)}) collective-permute-start(bf16[384,128]{1,0:T(8,128)(2,1)S(1)} %fusion.1.refs_1_.refs_0_), channel_id=1, source_target_pairs={{0,4},{1,5},{2,6},{3,7},{4,0},{5,1},{6,2},{7,3},{8,12},{9,13},{10,... | collective-permute-start | bytes 294920 | tf_op jit(solution)/shard_map/ppermute | solution.py:42
  114.3 8.2 %collective-permute-start.42 = (bf16[384,128]{1,0:T(8,128)(2,1)S(1)}, bf16[384,128]{1,0:T(8,128)(2,1)S(1)}, u32[]{:S(2)}, u32[]{:S(2)}) collective-permute-start(bf16[384,128]{1,0:T(8,128)(2,1)S(1)} %fusion.1.refs_1_.refs_0_), channel_id=1, source_target_pairs={{0,1},{1,0},{2,3},{3,2},{4,5},{5,4},{6,7},{7,6},{8,9},{9,8},{10,11... | collective-permute-start | bytes 294920 | tf_op jit(solution)/shard_map/ppermute | solution.py:31
  115.2 8.2 %collective-permute-start.59 = (bf16[384,128]{1,0:T(8,128)(2,1)S(1)}, bf16[384,128]{1,0:T(8,128)(2,1)S(1)}, u32[]{:S(2)}, u32[]{:S(2)}) collective-permute-start(bf16[384,128]{1,0:T(8,128)(2,1)S(1)} %collective-permute-done.57.refs_16_), channel_id=1, source_target_pairs={{0,8},{1,9},{2,10},{3,11},{4,12},{5,13},{6,14},{7,15},{8,0},{9,1},... | collective-permute-start | bytes 294920 | tf_op jit(solution)/shard_map/ppermute | solution.py:26
  137.5 7.6 %collective-permute-start.52 = (bf16[384,128]{1,0:T(8,128)(2,1)S(1)}, bf16[384,128]{1,0:T(8,128)(2,1)S(1)}, u32[]{:S(2)}, u32[]{:S(2)}) collective-permute-start(bf16[384,128]{1,0:T(8,128)(2,1)S(1)} %collective-permute-done.51.refs_10_), channel_id=1, source_target_pairs={{0,1},{1,0},{2,3},{3,2},{4,5},{5,4},{6,7},{7,6},{8,9},{9,8},{10,11... | collective-permute-start | bytes 294920 | tf_op jit(solution)/shard_map/ppermute | solution.py:31
  154.8 7.8 %collective-permute-start.77 = (bf16[2,384,128]{2,1,0:T(8,128)(2,1)S(1)}, bf16[2,384,128]{2,1,0:T(8,128)(2,1)S(1)}, u32[]{:S(2)}, u32[]{:S(2)}) collective-permute-start(bf16[2,384,128]{2,1,0:T(8,128)(2,1)S(1)} %get-tuple-element.67), channel_id=1, source_target_pairs={{0,8},{1,9},{2,10},{3,11},{4,12},{5,13},{6,14},{7,15},{8,0},{9,1},... | collective-permute-start | bytes 589832 | tf_op jit(solution)/shard_map/ppermute | solution.py:26
  156.6 9.6 %collective-permute-start.74 = (bf16[2,384,128]{2,1,0:T(8,128)(2,1)S(1)}, bf16[2,384,128]{2,1,0:T(8,128)(2,1)S(1)}, u32[]{:S(2)}, u32[]{:S(2)}) collective-permute-start(bf16[2,384,128]{2,1,0:T(8,128)(2,1)S(1)} %get-tuple-element.63), channel_id=1, source_target_pairs={{0,8},{1,9},{2,10},{3,11},{4,12},{5,13},{6,14},{7,15},{8,0},{9,1},... | collective-permute-start | bytes 589832 | tf_op jit(solution)/shard_map/ppermute | solution.py:26
  157.6 8.6 %collective-permute-start.83 = (bf16[2,384,128]{2,1,0:T(8,128)(2,1)S(1)}, bf16[2,384,128]{2,1,0:T(8,128)(2,1)S(1)}, u32[]{:S(2)}, u32[]{:S(2)}) collective-permute-start(bf16[2,384,128]{2,1,0:T(8,128)(2,1)S(1)} %get-tuple-element.64), channel_id=1, source_target_pairs={{0,16},{1,17},{2,18},{3,19},{4,20},{5,21},{6,22},{7,23},{8,24},{9,... | collective-permute-start | bytes 589832 | tf_op jit(solution)/shard_map/ppermute | solution.py:26
  158.7 10.8 %collective-permute-start.80 = (bf16[2,384,128]{2,1,0:T(8,128)(2,1)S(1)}, bf16[2,384,128]{2,1,0:T(8,128)(2,1)S(1)}, u32[]{:S(2)}, u32[]{:S(2)}) collective-permute-start(bf16[2,384,128]{2,1,0:T(8,128)(2,1)S(1)} %get-tuple-element.68), channel_id=1, source_target_pairs={{0,16},{1,17},{2,18},{3,19},{4,20},{5,21},{6,22},{7,23},{8,24},{9,... | collective-permute-start | bytes 589832 | tf_op jit(solution)/shard_map/ppermute | solution.py:26
  162.6 9.0 %collective-permute-start.78 = (bf16[1,384,128]{2,1,0:T(8,128)(2,1)S(1)}, bf16[1,384,128]{2,1,0:T(8,128)(2,1)S(1)}, u32[]{:S(2)}, u32[]{:S(2)}) collective-permute-start(bf16[1,384,128]{2,1,0:T(8,128)(2,1)S(1)} %add_convert_fusion.26), channel_id=1, source_target_pairs={{0,16},{1,17},{2,18},{3,19},{4,20},{5,21},{6,22},{7,23},{8,24},{9,... | collective-permute-start | bytes 294920 | tf_op jit(solution)/shard_map/ppermute | solution.py:26
  166.3 11.5 %collective-permute-start.75 = (bf16[1,384,128]{2,1,0:T(8,128)(2,1)S(1)}, bf16[1,384,128]{2,1,0:T(8,128)(2,1)S(1)}, u32[]{:S(2)}, u32[]{:S(2)}) collective-permute-start(bf16[1,384,128]{2,1,0:T(8,128)(2,1)S(1)} %get-tuple-element.61), channel_id=1, source_target_pairs={{0,16},{1,17},{2,18},{3,19},{4,20},{5,21},{6,22},{7,23},{8,24},{9,... | collective-permute-start | bytes 294920 | tf_op jit(solution)/shard_map/ppermute | solution.py:26
  173.0 8.8 %collective-permute-start.79 = (bf16[1,384,128]{2,1,0:T(8,128)(2,1)S(1)}, bf16[1,384,128]{2,1,0:T(8,128)(2,1)S(1)}, u32[]{:S(2)}, u32[]{:S(2)}) collective-permute-start(bf16[1,384,128]{2,1,0:T(8,128)(2,1)S(1)} %get-tuple-element.65), channel_id=1, source_target_pairs={{0,4},{1,5},{2,6},{3,7},{4,0},{5,1},{6,2},{7,3},{8,12},{9,13},{10,... | collective-permute-start | bytes 294920 | tf_op jit(solution)/shard_map/ppermute | solution.py:42
  186.8 8.3 %collective-permute-start.89 = (bf16[384,128]{1,0:T(8,128)(2,1)S(1)}, bf16[384,128]{1,0:T(8,128)(2,1)S(1)}, u32[]{:S(2)}, u32[]{:S(2)}) collective-permute-start(bf16[384,128]{1,0:T(8,128)(2,1)S(1)} %bitcast.13), channel_id=1, source_target_pairs={{0,4},{1,5},{2,6},{3,7},{4,0},{5,1},{6,2},{7,3},{8,12},{9,13},{10,... | collective-permute-start | bytes 294920 | tf_op jit(solution)/shard_map/ppermute | solution.py:42
  187.4 7.6 %collective-permute-start.87 = (bf16[384,128]{1,0:T(8,128)(2,1)S(1)}, bf16[384,128]{1,0:T(8,128)(2,1)S(1)}, u32[]{:S(2)}, u32[]{:S(2)}) collective-permute-start(bf16[384,128]{1,0:T(8,128)(2,1)S(1)} %bitcast.14), channel_id=1, source_target_pairs={{0,2},{1,3},{2,4},{3,5},{4,6},{5,7},{6,0},{7,1},{8,10},{9,11},{10,... | collective-permute-start | bytes 294920 | tf_op jit(solution)/shard_map/ppermute | solution.py:42
  187.4 8.7 %collective-permute-start.86 = (bf16[384,128]{1,0:T(8,128)(2,1)S(1)}, bf16[384,128]{1,0:T(8,128)(2,1)S(1)}, u32[]{:S(2)}, u32[]{:S(2)}) collective-permute-start(bf16[384,128]{1,0:T(8,128)(2,1)S(1)} %bitcast.15), channel_id=1, source_target_pairs={{0,1},{1,0},{2,3},{3,2},{4,5},{5,4},{6,7},{7,6},{8,9},{9,8},{10,11... | collective-permute-start | bytes 294920 | tf_op jit(solution)/shard_map/ppermute | solution.py:31
  187.7 8.7 %collective-permute-start.103 = (bf16[384,128]{1,0:T(8,128)(2,1)S(1)}, bf16[384,128]{1,0:T(8,128)(2,1)S(1)}, u32[]{:S(2)}, u32[]{:S(2)}) collective-permute-start(bf16[384,128]{1,0:T(8,128)(2,1)S(1)} %collective-permute-done.101.refs_17_), channel_id=1, source_target_pairs={{0,8},{1,9},{2,10},{3,11},{4,12},{5,13},{6,14},{7,15},{8,0},{9,1},... | collective-permute-start | bytes 294920 | tf_op jit(solution)/shard_map/ppermute | solution.py:26
  212.0 7.5 %collective-permute-start.96 = (bf16[384,128]{1,0:T(8,128)(2,1)S(1)}, bf16[384,128]{1,0:T(8,128)(2,1)S(1)}, u32[]{:S(2)}, u32[]{:S(2)}) collective-permute-start(bf16[384,128]{1,0:T(8,128)(2,1)S(1)} %collective-permute-done.95.refs_11_), channel_id=1, source_target_pairs={{0,1},{1,0},{2,3},{3,2},{4,5},{5,4},{6,7},{7,6},{8,9},{9,8},{10,11... | collective-permute-start | bytes 294920 | tf_op jit(solution)/shard_map/ppermute | solution.py:31
  231.9 7.8 %collective-permute-start.118 = (bf16[2,384,128]{2,1,0:T(8,128)(2,1)S(1)}, bf16[2,384,128]{2,1,0:T(8,128)(2,1)S(1)}, u32[]{:S(2)}, u32[]{:S(2)}) collective-permute-start(bf16[2,384,128]{2,1,0:T(8,128)(2,1)S(1)} %add_convert_fusion.1), channel_id=1, source_target_pairs={{0,8},{1,9},{2,10},{3,11},{4,12},{5,13},{6,14},{7,15},{8,0},{9,1},... | collective-permute-start | bytes 589832 | tf_op jit(solution)/shard_map/ppermute | solution.py:26
  232.5 10.9 %collective-permute-start.120 = (bf16[2,384,128]{2,1,0:T(8,128)(2,1)S(1)}, bf16[2,384,128]{2,1,0:T(8,128)(2,1)S(1)}, u32[]{:S(2)}, u32[]{:S(2)}) collective-permute-start(bf16[2,384,128]{2,1,0:T(8,128)(2,1)S(1)} %add_convert_fusion), channel_id=1, source_target_pairs={{0,8},{1,9},{2,10},{3,11},{4,12},{5,13},{6,14},{7,15},{8,0},{9,1},... | collective-permute-start | bytes 589832 | tf_op jit(solution)/shard_map/ppermute | solution.py:26
  254.2 9.6 %collective-permute-start.127 = (bf16[384,128]{1,0:T(8,128)(2,1)S(1)}, bf16[384,128]{1,0:T(8,128)(2,1)S(1)}, u32[]{:S(2)}, u32[]{:S(2)}) collective-permute-start(bf16[384,128]{1,0:T(8,128)(2,1)S(1)} %bitcast.20), channel_id=1, source_target_pairs={{0,4},{1,5},{2,6},{3,7},{4,0},{5,1},{6,2},{7,3},{8,12},{9,13},{10,... | collective-permute-start | bytes 294920 | tf_op jit(solution)/shard_map/ppermute | solution.py:42
  254.8 9.0 %collective-permute-start.125 = (bf16[384,128]{1,0:T(8,128)(2,1)S(1)}, bf16[384,128]{1,0:T(8,128)(2,1)S(1)}, u32[]{:S(2)}, u32[]{:S(2)}) collective-permute-start(bf16[384,128]{1,0:T(8,128)(2,1)S(1)} %bitcast.21), channel_id=1, source_target_pairs={{0,2},{1,3},{2,4},{3,5},{4,6},{5,7},{6,0},{7,1},{8,10},{9,11},{10,... | collective-permute-start | bytes 294920 | tf_op jit(solution)/shard_map/ppermute | solution.py:42
  254.8 10.7 %collective-permute-start.124 = (bf16[384,128]{1,0:T(8,128)(2,1)S(1)}, bf16[384,128]{1,0:T(8,128)(2,1)S(1)}, u32[]{:S(2)}, u32[]{:S(2)}) collective-permute-start(bf16[384,128]{1,0:T(8,128)(2,1)S(1)} %bitcast.22), channel_id=1, source_target_pairs={{0,1},{1,0},{2,3},{3,2},{4,5},{5,4},{6,7},{7,6},{8,9},{9,8},{10,11... | collective-permute-start | bytes 294920 | tf_op jit(solution)/shard_map/ppermute | solution.py:31
  255.4 10.5 %collective-permute-start.132 = (bf16[384,128]{1,0:T(8,128)(2,1)S(1)}, bf16[384,128]{1,0:T(8,128)(2,1)S(1)}, u32[]{:S(2)}, u32[]{:S(2)}) collective-permute-start(bf16[384,128]{1,0:T(8,128)(2,1)S(1)} %collective-permute-done.131.refs_9_), channel_id=1, source_target_pairs={{0,1},{1,0},{2,3},{3,2},{4,5},{5,4},{6,7},{7,6},{8,9},{9,8},{10,11... | collective-permute-start | bytes 294920 | tf_op jit(solution)/shard_map/ppermute | solution.py:31
  257.4 8.5 %collective-permute-start.137 = (bf16[384,128]{1,0:T(8,128)(2,1)S(1)}, bf16[384,128]{1,0:T(8,128)(2,1)S(1)}, u32[]{:S(2)}, u32[]{:S(2)}) collective-permute-start(bf16[384,128]{1,0:T(8,128)(2,1)S(1)} %collective-permute-done.129.refs_7_), channel_id=1, source_target_pairs={{0,8},{1,9},{2,10},{3,11},{4,12},{5,13},{6,14},{7,15},{8,0},{9,1},... | collective-permute-start | bytes 294920 | tf_op jit(solution)/shard_map/ppermute | solution.py:26
  265.9 7.7 %collective-permute-start.128 = (bf16[384,128]{1,0:T(8,128)(2,1)S(1)}, bf16[384,128]{1,0:T(8,128)(2,1)S(1)}, u32[]{:S(2)}, u32[]{:S(2)}) collective-permute-start(bf16[384,128]{1,0:T(8,128)(2,1)S(1)} %collective-permute-done.127.refs_5_), channel_id=1, source_target_pairs={{0,1},{1,0},{2,3},{3,2},{4,5},{5,4},{6,7},{7,6},{8,9},{9,8},{10,11... | collective-permute-start | bytes 294920 | tf_op jit(solution)/shard_map/ppermute | solution.py:31
  265.9 7.7 %collective-permute-start.126 = (bf16[384,128]{1,0:T(8,128)(2,1)S(1)}, bf16[384,128]{1,0:T(8,128)(2,1)S(1)}, u32[]{:S(2)}, u32[]{:S(2)}) collective-permute-start(bf16[384,128]{1,0:T(8,128)(2,1)S(1)} %collective-permute-done.125.refs_3_), channel_id=1, source_target_pairs={{0,1},{1,0},{2,3},{3,2},{4,5},{5,4},{6,7},{7,6},{8,9},{9,8},{10,11... | collective-permute-start | bytes 294920 | tf_op jit(solution)/shard_map/ppermute | solution.py:31
  280.8 7.6 %collective-permute-start.143 = (bf16[1,384,128]{2,1,0:T(8,128)(2,1)S(1)}, bf16[1,384,128]{2,1,0:T(8,128)(2,1)S(1)}, u32[]{:S(2)}, u32[]{:S(2)}) collective-permute-start(bf16[1,384,128]{2,1,0:T(8,128)(2,1)S(1)} %add_convert_fusion.13), channel_id=1, source_target_pairs={{0,2},{1,3},{2,4},{3,5},{4,6},{5,7},{6,0},{7,1},{8,10},{9,11},{10,... | collective-permute-start | bytes 294920 | tf_op jit(solution)/shard_map/ppermute | solution.py:42
  282.1 9.9 %collective-permute-start.141 = (bf16[1,384,128]{2,1,0:T(8,128)(2,1)S(1)}, bf16[1,384,128]{2,1,0:T(8,128)(2,1)S(1)}, u32[]{:S(2)}, u32[]{:S(2)}) collective-permute-start(bf16[1,384,128]{2,1,0:T(8,128)(2,1)S(1)} %get-tuple-element.81), channel_id=1, source_target_pairs={{0,4},{1,5},{2,6},{3,7},{4,0},{5,1},{6,2},{7,3},{8,12},{9,13},{10,... | collective-permute-start | bytes 294920 | tf_op jit(solution)/shard_map/ppermute | solution.py:42
  282.2 9.8 %collective-permute-start.142 = (bf16[1,384,128]{2,1,0:T(8,128)(2,1)S(1)}, bf16[1,384,128]{2,1,0:T(8,128)(2,1)S(1)}, u32[]{:S(2)}, u32[]{:S(2)}) collective-permute-start(bf16[1,384,128]{2,1,0:T(8,128)(2,1)S(1)} %get-tuple-element.82), channel_id=1, source_target_pairs={{0,6},{1,7},{2,0},{3,1},{4,2},{5,3},{6,4},{7,5},{8,14},{9,15},{10,... | collective-permute-start | bytes 294920 | tf_op jit(solution)/shard_map/ppermute | solution.py:42
  (99 other events, 577.1 us)
where the time goes:
time: 293 us
  waiting for transfers between devices  137 us (47%)
  starting transfers between devices  97.3 us (33%)
  Pallas kernels  53 us (18%)
    ppermute x52, waiting for transfers between devices, swap_leaf(): return lax.ppermute(value, AXES, pairs)  68.7 us
    ppermute x30, waiting for transfers between devices, shift_depth(): return lax.ppermute(value, AXES, pairs)  59.2 us
    ppermute x52, starting transfers between devices, swap_leaf(): return lax.ppermute(value, AXES, pairs)  54.4 us
    pallas_call x5, Pallas kernels, run_level(): pl.pallas_call(functools.partial(kernel_body, plan), out_shape=out_shape,...  40.7 us
    ppermute x30, starting transfers between devices, shift_depth(): return lax.ppermute(value, AXES, pairs)  34.1 us
    pallas_call x4, Pallas kernels, load(): pl.pallas_call(functools.partial(load_kernel, count), out_shape=out_shape...  12.3 us
    ppermute x62, waiting for transfers between devices, swap_core(): return lax.ppermute(value, AXES, [(i, i ^ 1) for i in range(count)])  9.28 us
    ppermute x62, starting transfers between devices, swap_core(): return lax.ppermute(value, AXES, [(i, i ^ 1) for i in range(count)])  8.76 us
  transfers between devices with their start and end apart: 144, of which 65 were waited for; matrix products, arithmetic and copies ran while one was open for 1% of the time, Pallas kernels for 4%

commit v1 on v0

--- a/solution.py
+++ b/solution.py
@@ -370,10 +370,11 @@
     lists = (slots_low, slots_mid)
     height = len(inverses)
     leaf_at = lax.axis_index("leaf")
-    slot_rows = [
-        lax.dynamic_index_in_dim(lists[level], leaf_at >> level, 0, keepdims=False)
-        for level in range(height - 1)
-    ]
+    slot_rows = []
+    for level in range(height - 1):
+        slot_rows.append(
+            lax.dynamic_index_in_dim(lists[level], leaf_at >> level, 0, keepdims=False)
+        )
     solved = []
     local_rows = right_sides[0]
     for level in range(height - 1):

time: 293 us -> 293 us (level)
  no operation moved by 1% of the time
where the time goes in v1:
time: 293 us
  waiting for transfers between devices  137 us (47%)
  starting transfers between devices  97.3 us (33%)
  Pallas kernels  53 us (18%)
    ppermute x52, waiting for transfers between devices, swap_leaf(): return lax.ppermute(value, AXES, pairs)  68.7 us
    ppermute x30, waiting for transfers between devices, shift_depth(): return lax.ppermute(value, AXES, pairs)  59.2 us
    ppermute x52, starting transfers between devices, swap_leaf(): return lax.ppermute(value, AXES, pairs)  54.4 us
    pallas_call x5, Pallas kernels, run_level(): pl.pallas_call(functools.partial(kernel_body, plan), out_shape=out_shape,...  40.7 us
    ppermute x30, starting transfers between devices, shift_depth(): return lax.ppermute(value, AXES, pairs)  34.1 us
    pallas_call x4, Pallas kernels, load(): pl.pallas_call(functools.partial(load_kernel, count), out_shape=out_shape...  12.3 us
    ppermute x62, waiting for transfers between devices, swap_core(): return lax.ppermute(value, AXES, [(i, i ^ 1) for i in range(count)])  9.28 us
    ppermute x62, starting transfers between devices, swap_core(): return lax.ppermute(value, AXES, [(i, i ^ 1) for i in range(count)])  8.76 us
  transfers between devices with their start and end apart: 144, of which 65 were waited for; matrix products, arithmetic and copies ran while one was open for 1% of the time, Pallas kernels for 4%

profile of v1, /device:TPU:0, one launch (start us, length us, event | category | flops | bytes accessed | tf_op | source)
XLA Modules:
  0.0 292.8 jit_solution(18217838480738223435)
XLA Ops:
  0.9 5.1 %collective-permute-start.5 = (bf16[384,128]{1,0:T(8,128)(2,1)S(1)}, bf16[384,128]{1,0:T(8,128)(2,1)S(1)}, u32[]{:S(2)}, u32[]{:S(2)}) collective-permute-start(bf16[384,128]{1,0:T(8,128)(2,1)S(1)} %slice_bitcast_fusion.refs_2_.refs_1_), channel_id=1, source_target_pairs={{0,6},{1,7},{2,0},{3,1},{4,2},{5,3},{6,4},{7,5},{8,14},{9,15},{10,... | collective-permute-start | bytes 294920 | tf_op jit(solution)/shard_map/ppermute | solution.py:42
  7.0 2.2 collective-permute-done.5.refs_7_
  9.2 5.6 %collective-permute-done.3.refs_5_ = bf16[384,128]{1,0:T(8,128)(2,1)S(1)} collective-permute-done((bf16[384,128]{1,0:T(8,128)(2,1)S(1)}, bf16[384,128]{1,0:T(8,128)(2,1)S(1)}, u32[]{:S(2)}, u32[]{:S(2)}) %collective-permute-start.3) | collective-permute-done | bytes 98336 | tf_op jit(solution)/shard_map/ppermute | solution.py:42
  16.1 2.4 shard_map.82
  18.5 5.5 %shard_map.83 = (bf16[384,128]{1,0:T(8,128)(2,1)S(1)}, bf16[4,384,128]{2,1,0:T(8,128)(2,1)S(1)}, bf16[4,384,128]{2,1,0:T(8,128)(2,1)S(1)}, bf16[4,384,128]{2,1,0:T(8,128)(2,1)S(1)}, bf16[4,384,128]{2,1,0:T(8,128)(2,1)S(1)}) custom-call(s32[3072]{0:T(1024)S(1)} %bitcast.27, bf16[384,128]{1,0:T(8,128)(2,1)S(1)} %slice_bitcast_fusion.refs_2_.refs_1_, ...), custom_call_target="tpu_custom_call" | custom-call | tf_op jit(solution)/shard_map/pallas_call | solution.py:352
  28.1 5.6 %collective-permute-done.8 = bf16[2,384,128]{2,1,0:T(8,128)(2,1)S(1)} collective-permute-done((bf16[2,384,128]{2,1,0:T(8,128)(2,1)S(1)}, bf16[2,384,128]{2,1,0:T(8,128)(2,1)S(1)}, u32[]{:S(2)}, u32[]{:S(2)}) %collective-permute-start.8) | collective-permute-done | bytes 196640 | tf_op jit(solution)/shard_map/ppermute | solution.py:26
  33.8 3.3 %collective-permute-done.10 = bf16[2,384,128]{2,1,0:T(8,128)(2,1)S(1)} collective-permute-done((bf16[2,384,128]{2,1,0:T(8,128)(2,1)S(1)}, bf16[2,384,128]{2,1,0:T(8,128)(2,1)S(1)}, u32[]{:S(2)}, u32[]{:S(2)}) %collective-permute-start.10) | collective-permute-done | bytes 196640 | tf_op jit(solution)/shard_map/ppermute | solution.py:26
  37.2 2.2 collective-permute-start.11
  40.6 4.1 %collective-permute-done.11 = bf16[1,384,128]{2,1,0:T(8,128)(2,1)S(1)} collective-permute-done((bf16[1,384,128]{2,1,0:T(8,128)(2,1)S(1)}, bf16[1,384,128]{2,1,0:T(8,128)(2,1)S(1)}, u32[]{:S(2)}, u32[]{:S(2)}) %collective-permute-start.11) | collective-permute-done | bytes 98336 | tf_op jit(solution)/shard_map/ppermute | solution.py:42
  47.0 3.2 %collective-permute-start.19 = (bf16[384,128]{1,0:T(8,128)(2,1)S(1)}, bf16[384,128]{1,0:T(8,128)(2,1)S(1)}, u32[]{:S(2)}, u32[]{:S(2)}) collective-permute-start(bf16[384,128]{1,0:T(8,128)(2,1)S(1)} %fusion.refs_1_), channel_id=1, source_target_pairs={{0,6},{1,7},{2,0},{3,1},{4,2},{5,3},{6,4},{7,5},{8,14},{9,15},{10,... | collective-permute-start | bytes 294920 | tf_op jit(solution)/shard_map/ppermute | solution.py:42
  53.4 5.4 %collective-permute-done.17.refs_5_ = bf16[384,128]{1,0:T(8,128)(2,1)S(1)} collective-permute-done((bf16[384,128]{1,0:T(8,128)(2,1)S(1)}, bf16[384,128]{1,0:T(8,128)(2,1)S(1)}, u32[]{:S(2)}, u32[]{:S(2)}) %collective-permute-start.17) | collective-permute-done | bytes 98336 | tf_op jit(solution)/shard_map/ppermute | solution.py:42
  61.4 3.0 %collective-permute-done.25.refs_13_ = bf16[384,128]{1,0:T(8,128)(2,1)S(1)} collective-permute-done((bf16[384,128]{1,0:T(8,128)(2,1)S(1)}, bf16[384,128]{1,0:T(8,128)(2,1)S(1)}, u32[]{:S(2)}, u32[]{:S(2)}) %collective-permute-start.25) | collective-permute-done | bytes 98336 | tf_op jit(solution)/shard_map/ppermute | solution.py:26
  67.4 12.2 %shard_map.84 = (bf16[384,128]{1,0:T(8,128)(2,1)S(1)}, bf16[8,384,128]{2,1,0:T(8,128)(2,1)S(1)}, bf16[8,384,128]{2,1,0:T(8,128)(2,1)S(1)}, bf16[8,384,128]{2,1,0:T(8,128)(2,1)S(1)}, bf16[8,384,128]{2,1,0:T(8,128)(2,1)S(1)}) custom-call(s32[6144]{0:T(1024)S(1)} %bitcast.25, bf16[384,128]{1,0:T(8,128)(2,1)S(1)} %fusion.refs_1_, ...), custom_call_target="tpu_custom_call" | custom-call | tf_op jit(solution)/shard_map/pallas_call | solution.py:352
  86.4 3.5 %collective-permute-done.33 = bf16[2,384,128]{2,1,0:T(8,128)(2,1)S(1)} collective-permute-done((bf16[2,384,128]{2,1,0:T(8,128)(2,1)S(1)}, bf16[2,384,128]{2,1,0:T(8,128)(2,1)S(1)}, u32[]{:S(2)}, u32[]{:S(2)}) %collective-permute-start.33) | collective-permute-done | bytes 196640 | tf_op jit(solution)/shard_map/ppermute | solution.py:26
  96.4 1.8 collective-permute-done.34
  104.7 2.6 collective-permute-done.41
  107.4 2.1 collective-permute-done.35
  117.9 3.2 %collective-permute-done.45.refs_4_ = bf16[384,128]{1,0:T(8,128)(2,1)S(1)} collective-permute-done((bf16[384,128]{1,0:T(8,128)(2,1)S(1)}, bf16[384,128]{1,0:T(8,128)(2,1)S(1)}, u32[]{:S(2)}, u32[]{:S(2)}) %collective-permute-start.45) | collective-permute-done | bytes 98336 | tf_op jit(solution)/shard_map/ppermute | solution.py:42
  128.0 2.2 collective-permute-start.51
  132.9 2.0 collective-permute-start.67
  138.9 2.4 collective-permute-done.63.refs_22_
  141.3 3.8 %shard_map.85.refs_32_ = bf16[384,12288]{1,0:T(8,128)(2,1)S(1)} custom-call(bf16[384,12288]{1,0:T(8,128)(2,1)} %refs_0_.5, bf16[384,128]{1,0:T(8,128)(2,1)S(1)} %fusion.1.refs_1_.refs_0_), custom_call_target="tpu_custom_call" | custom-call | bytes 18874368 | tf_op jit(solution)/shard_map/pallas_call | solution.py:296
  145.1 7.0 %shard_map.86 = (bf16[8,384,128]{2,1,0:T(8,128)(2,1)S(1)}, bf16[8,384,128]{2,1,0:T(8,128)(2,1)S(1)}, bf16[8,384,128]{2,1,0:T(8,128)(2,1)S(1)}, bf16[8,384,128]{2,1,0:T(8,128)(2,1)S(1)}) custom-call(bf16[384,128]{1,0:T(8,128)(2,1)S(1)} %fusion.1.refs_1_.refs_0_, bf16[384,128]{1,0:T(8,128)(2,1)S(1)} %collective-permute-done.42.refs_1_, ...), custom_call_target="tpu_custom_call" | custom-call | tf_op jit(solution)/shard_map/pallas_call | solution.py:352
  152.8 1.8 collective-permute-done.76
  159.6 3.0 %collective-permute-done.77 = bf16[2,384,128]{2,1,0:T(8,128)(2,1)S(1)} collective-permute-done((bf16[2,384,128]{2,1,0:T(8,128)(2,1)S(1)}, bf16[2,384,128]{2,1,0:T(8,128)(2,1)S(1)}, u32[]{:S(2)}, u32[]{:S(2)}) %collective-permute-start.77) | collective-permute-done | bytes 196640 | tf_op jit(solution)/shard_map/ppermute | solution.py:26
  163.6 2.6 collective-permute-done.74
  169.6 2.1 collective-permute-done.78
  173.0 1.8 collective-permute-start.79
  179.5 2.3 collective-permute-done.79
  184.2 2.5 collective-permute-start.91
  189.1 6.0 %collective-permute-done.89.refs_5_ = bf16[384,128]{1,0:T(8,128)(2,1)S(1)} collective-permute-done((bf16[384,128]{1,0:T(8,128)(2,1)S(1)}, bf16[384,128]{1,0:T(8,128)(2,1)S(1)}, u32[]{:S(2)}, u32[]{:S(2)}) %collective-permute-start.89) | collective-permute-done | bytes 98336 | tf_op jit(solution)/shard_map/ppermute | solution.py:42
  203.7 2.7 collective-permute-done.105.refs_21_
  208.1 3.0 %collective-permute-done.115.refs_31_ = bf16[384,128]{1,0:T(8,128)(2,1)S(1)} collective-permute-done((bf16[384,128]{1,0:T(8,128)(2,1)S(1)}, bf16[384,128]{1,0:T(8,128)(2,1)S(1)}, u32[]{:S(2)}, u32[]{:S(2)}) %collective-permute-start.115) | collective-permute-done | bytes 98336 | tf_op jit(solution)/shard_map/ppermute | solution.py:26
  213.2 2.5 collective-permute-done.107.refs_23_
  215.6 3.8 %shard_map.87 = (bf16[384,6144]{1,0:T(8,128)(2,1)S(1)}, bf16[384,6144]{1,0:T(8,128)(2,1)S(1)}) custom-call(bf16[384,6144]{1,0:T(8,128)(2,1)} %refs_0_.6, bf16[384,6144]{1,0:T(8,128)(2,1)} %refs_1_.4, bf16[384,128]{1,0:T(8,128)(2,1)S(1)} %bitcast.16), custom_call_target="tpu_custom_call" | custom-call | bytes 18874368 | tf_op jit(solution)/shard_map/pallas_call | solution.py:296
  219.5 10.4 %shard_map.88 = (bf16[4,384,128]{2,1,0:T(8,128)(2,1)S(1)}, bf16[4,384,128]{2,1,0:T(8,128)(2,1)S(1)}, bf16[4,384,128]{2,1,0:T(8,128)(2,1)S(1)}, bf16[4,384,128]{2,1,0:T(8,128)(2,1)S(1)}) custom-call(s32[6144]{0:T(1024)S(1)} %bitcast.26, bf16[384,128]{1,0:T(8,128)(2,1)S(1)} %bitcast.17, bf16[384,128]{1,0:T(8,128)(2,1)S(1)} %collective-permute-done.86.refs_2_, ...), custom_call_target="tpu_custom_call" | custom-call | tf_op jit(solution)/shard_map/pallas_call | solution.py:352
  234.1 5.6 %collective-permute-done.118 = bf16[2,384,128]{2,1,0:T(8,128)(2,1)S(1)} collective-permute-done((bf16[2,384,128]{2,1,0:T(8,128)(2,1)S(1)}, bf16[2,384,128]{2,1,0:T(8,128)(2,1)S(1)}, u32[]{:S(2)}, u32[]{:S(2)}) %collective-permute-start.118) | collective-permute-done | bytes 196640 | tf_op jit(solution)/shard_map/ppermute | solution.py:26
  239.9 3.5 %collective-permute-done.120 = bf16[2,384,128]{2,1,0:T(8,128)(2,1)S(1)} collective-permute-done((bf16[2,384,128]{2,1,0:T(8,128)(2,1)S(1)}, bf16[2,384,128]{2,1,0:T(8,128)(2,1)S(1)}, u32[]{:S(2)}, u32[]{:S(2)}) %collective-permute-start.120) | collective-permute-done | bytes 196640 | tf_op jit(solution)/shard_map/ppermute | solution.py:26
  247.1 3.5 %collective-permute-done.121 = bf16[1,384,128]{2,1,0:T(8,128)(2,1)S(1)} collective-permute-done((bf16[1,384,128]{2,1,0:T(8,128)(2,1)S(1)}, bf16[1,384,128]{2,1,0:T(8,128)(2,1)S(1)}, u32[]{:S(2)}, u32[]{:S(2)}) %collective-permute-start.121) | collective-permute-done | bytes 98336 | tf_op jit(solution)/shard_map/ppermute | solution.py:42
  251.1 3.2 %collective-permute-start.129 = (bf16[384,128]{1,0:T(8,128)(2,1)S(1)}, bf16[384,128]{1,0:T(8,128)(2,1)S(1)}, u32[]{:S(2)}, u32[]{:S(2)}) collective-permute-start(bf16[384,128]{1,0:T(8,128)(2,1)S(1)} %bitcast.19), channel_id=1, source_target_pairs={{0,6},{1,7},{2,0},{3,1},{4,2},{5,3},{6,4},{7,5},{8,14},{9,15},{10,... | collective-permute-start | bytes 294920 | tf_op jit(solution)/shard_map/ppermute | solution.py:42
  255.4 2.0 collective-permute-done.129.refs_7_
  258.9 4.9 %collective-permute-done.127.refs_5_ = bf16[384,128]{1,0:T(8,128)(2,1)S(1)} collective-permute-done((bf16[384,128]{1,0:T(8,128)(2,1)S(1)}, bf16[384,128]{1,0:T(8,128)(2,1)S(1)}, u32[]{:S(2)}, u32[]{:S(2)}) %collective-permute-start.127) | collective-permute-done | bytes 98336 | tf_op jit(solution)/shard_map/ppermute | solution.py:42
  266.4 3.0 %collective-permute-done.135.refs_13_ = bf16[384,128]{1,0:T(8,128)(2,1)S(1)} collective-permute-done((bf16[384,128]{1,0:T(8,128)(2,1)S(1)}, bf16[384,128]{1,0:T(8,128)(2,1)S(1)}, u32[]{:S(2)}, u32[]{:S(2)}) %collective-permute-start.135) | collective-permute-done | bytes 98336 | tf_op jit(solution)/shard_map/ppermute | solution.py:26
  271.1 2.4 shard_map.89
  273.6 5.5 %shard_map.90 = (bf16[2,384,128]{2,1,0:T(8,128)(2,1)S(1)}, bf16[2,384,128]{2,1,0:T(8,128)(2,1)S(1)}, bf16[2,384,128]{2,1,0:T(8,128)(2,1)S(1)}, bf16[2,384,128]{2,1,0:T(8,128)(2,1)S(1)}) custom-call(s32[3072]{0:T(1024)S(1)} %bitcast.28, bf16[384,128]{1,0:T(8,128)(2,1)S(1)} %bitcast.24, bf16[384,128]{1,0:T(8,128)(2,1)S(1)} %collective-permute-done.124.refs_2_, ...), custom_call_target="tpu_custom_call" | custom-call | tf_op jit(solution)/shard_map/pallas_call | solution.py:352
  282.2 2.7 collective-permute-start.142
  284.8 3.5 %collective-permute-done.143 = bf16[1,384,128]{2,1,0:T(8,128)(2,1)S(1)} collective-permute-done((bf16[1,384,128]{2,1,0:T(8,128)(2,1)S(1)}, bf16[1,384,128]{2,1,0:T(8,128)(2,1)S(1)}, u32[]{:S(2)}, u32[]{:S(2)}) %collective-permute-start.143) | collective-permute-done | bytes 98336 | tf_op jit(solution)/shard_map/ppermute | solution.py:42
  288.4 3.6 %collective-permute-done.141 = bf16[1,384,128]{2,1,0:T(8,128)(2,1)S(1)} collective-permute-done((bf16[1,384,128]{2,1,0:T(8,128)(2,1)S(1)}, bf16[1,384,128]{2,1,0:T(8,128)(2,1)S(1)}, u32[]{:S(2)}, u32[]{:S(2)}) %collective-permute-start.141) | collective-permute-done | bytes 98336 | tf_op jit(solution)/shard_map/ppermute | solution.py:42
  (288 shorter events, 113.8 us)
Async XLA Ops:
  0.9 8.3 %collective-permute-start.5 = (bf16[384,128]{1,0:T(8,128)(2,1)S(1)}, bf16[384,128]{1,0:T(8,128)(2,1)S(1)}, u32[]{:S(2)}, u32[]{:S(2)}) collective-permute-start(bf16[384,128]{1,0:T(8,128)(2,1)S(1)} %slice_bitcast_fusion.refs_2_.refs_1_), channel_id=1, source_target_pairs={{0,6},{1,7},{2,0},{3,1},{4,2},{5,3},{6,4},{7,5},{8,14},{9,15},{10,... | collective-permute-start | bytes 294920 | tf_op jit(solution)/shard_map/ppermute | solution.py:42
  6.0 8.8 %collective-permute-start.3 = (bf16[384,128]{1,0:T(8,128)(2,1)S(1)}, bf16[384,128]{1,0:T(8,128)(2,1)S(1)}, u32[]{:S(2)}, u32[]{:S(2)}) collective-permute-start(bf16[384,128]{1,0:T(8,128)(2,1)S(1)} %slice_bitcast_fusion.refs_2_.refs_1_), channel_id=1, source_target_pairs={{0,4},{1,5},{2,6},{3,7},{4,0},{5,1},{6,2},{7,3},{8,12},{9,13},{10,... | collective-permute-start | bytes 294920 | tf_op jit(solution)/shard_map/ppermute | solution.py:42
  6.0 8.8 %collective-permute-start.1 = (bf16[384,128]{1,0:T(8,128)(2,1)S(1)}, bf16[384,128]{1,0:T(8,128)(2,1)S(1)}, u32[]{:S(2)}, u32[]{:S(2)}) collective-permute-start(bf16[384,128]{1,0:T(8,128)(2,1)S(1)} %slice_bitcast_fusion.refs_2_.refs_1_), channel_id=1, source_target_pairs={{0,2},{1,3},{2,4},{3,5},{4,6},{5,7},{6,0},{7,1},{8,10},{9,11},{10,... | collective-permute-start | bytes 294920 | tf_op jit(solution)/shard_map/ppermute | solution.py:42
  7.0 11.5 %collective-permute-start = (bf16[384,128]{1,0:T(8,128)(2,1)S(1)}, bf16[384,128]{1,0:T(8,128)(2,1)S(1)}, u32[]{:S(2)}, u32[]{:S(2)}) collective-permute-start(bf16[384,128]{1,0:T(8,128)(2,1)S(1)} %slice_bitcast_fusion.refs_2_.refs_1_), channel_id=1, source_target_pairs={{0,1},{1,0},{2,3},{3,2},{4,5},{5,4},{6,7},{7,6},{8,9},{9,8},{10,11... | collective-permute-start | bytes 294920 | tf_op jit(solution)/shard_map/ppermute | solution.py:31
  9.2 9.3 %collective-permute-start.6 = (bf16[384,128]{1,0:T(8,128)(2,1)S(1)}, bf16[384,128]{1,0:T(8,128)(2,1)S(1)}, u32[]{:S(2)}, u32[]{:S(2)}) collective-permute-start(bf16[384,128]{1,0:T(8,128)(2,1)S(1)} %collective-permute-done.5.refs_7_), channel_id=1, source_target_pairs={{0,1},{1,0},{2,3},{3,2},{4,5},{5,4},{6,7},{7,6},{8,9},{9,8},{10,11... | collective-permute-start | bytes 294920 | tf_op jit(solution)/shard_map/ppermute | solution.py:31
  25.9 7.8 %collective-permute-start.8 = (bf16[2,384,128]{2,1,0:T(8,128)(2,1)S(1)}, bf16[2,384,128]{2,1,0:T(8,128)(2,1)S(1)}, u32[]{:S(2)}, u32[]{:S(2)}) collective-permute-start(bf16[2,384,128]{2,1,0:T(8,128)(2,1)S(1)} %add_convert_fusion.11), channel_id=1, source_target_pairs={{0,8},{1,9},{2,10},{3,11},{4,12},{5,13},{6,14},{7,15},{8,0},{9,1},... | collective-permute-start | bytes 589832 | tf_op jit(solution)/shard_map/ppermute | solution.py:26
  27.5 9.6 %collective-permute-start.10 = (bf16[2,384,128]{2,1,0:T(8,128)(2,1)S(1)}, bf16[2,384,128]{2,1,0:T(8,128)(2,1)S(1)}, u32[]{:S(2)}, u32[]{:S(2)}) collective-permute-start(bf16[2,384,128]{2,1,0:T(8,128)(2,1)S(1)} %add_convert_fusion.10), channel_id=1, source_target_pairs={{0,8},{1,9},{2,10},{3,11},{4,12},{5,13},{6,14},{7,15},{8,0},{9,1},... | collective-permute-start | bytes 589832 | tf_op jit(solution)/shard_map/ppermute | solution.py:26
  37.2 7.5 %collective-permute-start.11 = (bf16[1,384,128]{2,1,0:T(8,128)(2,1)S(1)}, bf16[1,384,128]{2,1,0:T(8,128)(2,1)S(1)}, u32[]{:S(2)}, u32[]{:S(2)}) collective-permute-start(bf16[1,384,128]{2,1,0:T(8,128)(2,1)S(1)} %get-tuple-element.79), channel_id=1, source_target_pairs={{0,4},{1,5},{2,6},{3,7},{4,0},{5,1},{6,2},{7,3},{8,12},{9,13},{10,... | collective-permute-start | bytes 294920 | tf_op jit(solution)/shard_map/ppermute | solution.py:42
  50.2 8.6 %collective-permute-start.17 = (bf16[384,128]{1,0:T(8,128)(2,1)S(1)}, bf16[384,128]{1,0:T(8,128)(2,1)S(1)}, u32[]{:S(2)}, u32[]{:S(2)}) collective-permute-start(bf16[384,128]{1,0:T(8,128)(2,1)S(1)} %fusion.refs_1_), channel_id=1, source_target_pairs={{0,4},{1,5},{2,6},{3,7},{4,0},{5,1},{6,2},{7,3},{8,12},{9,13},{10,... | collective-permute-start | bytes 294920 | tf_op jit(solution)/shard_map/ppermute | solution.py:42
  50.2 8.6 %collective-permute-start.15 = (bf16[384,128]{1,0:T(8,128)(2,1)S(1)}, bf16[384,128]{1,0:T(8,128)(2,1)S(1)}, u32[]{:S(2)}, u32[]{:S(2)}) collective-permute-start(bf16[384,128]{1,0:T(8,128)(2,1)S(1)} %fusion.refs_1_), channel_id=1, source_target_pairs={{0,2},{1,3},{2,4},{3,5},{4,6},{5,7},{6,0},{7,1},{8,10},{9,11},{10,... | collective-permute-start | bytes 294920 | tf_op jit(solution)/shard_map/ppermute | solution.py:42
  50.8 8.6 %collective-permute-start.14 = (bf16[384,128]{1,0:T(8,128)(2,1)S(1)}, bf16[384,128]{1,0:T(8,128)(2,1)S(1)}, u32[]{:S(2)}, u32[]{:S(2)}) collective-permute-start(bf16[384,128]{1,0:T(8,128)(2,1)S(1)} %fusion.refs_1_), channel_id=1, source_target_pairs={{0,1},{1,0},{2,3},{3,2},{4,5},{5,4},{6,7},{7,6},{8,9},{9,8},{10,11... | collective-permute-start | bytes 294920 | tf_op jit(solution)/shard_map/ppermute | solution.py:31
  50.8 10.1 %collective-permute-start.22 = (bf16[384,128]{1,0:T(8,128)(2,1)S(1)}, bf16[384,128]{1,0:T(8,128)(2,1)S(1)}, u32[]{:S(2)}, u32[]{:S(2)}) collective-permute-start(bf16[384,128]{1,0:T(8,128)(2,1)S(1)} %collective-permute-done.21.refs_9_), channel_id=1, source_target_pairs={{0,1},{1,0},{2,3},{3,2},{4,5},{5,4},{6,7},{7,6},{8,9},{9,8},{10,11... | collective-permute-start | bytes 294920 | tf_op jit(solution)/shard_map/ppermute | solution.py:31
  52.9 8.0 %collective-permute-start.27 = (bf16[384,128]{1,0:T(8,128)(2,1)S(1)}, bf16[384,128]{1,0:T(8,128)(2,1)S(1)}, u32[]{:S(2)}, u32[]{:S(2)}) collective-permute-start(bf16[384,128]{1,0:T(8,128)(2,1)S(1)} %collective-permute-done.19.refs_7_), channel_id=1, source_target_pairs={{0,8},{1,9},{2,10},{3,11},{4,12},{5,13},{6,14},{7,15},{8,0},{9,1},... | collective-permute-start | bytes 294920 | tf_op jit(solution)/shard_map/ppermute | solution.py:26
  82.1 7.8 %collective-permute-start.33 = (bf16[2,384,128]{2,1,0:T(8,128)(2,1)S(1)}, bf16[2,384,128]{2,1,0:T(8,128)(2,1)S(1)}, u32[]{:S(2)}, u32[]{:S(2)}) collective-permute-start(bf16[2,384,128]{2,1,0:T(8,128)(2,1)S(1)} %get-tuple-element.75), channel_id=1, source_target_pairs={{0,8},{1,9},{2,10},{3,11},{4,12},{5,13},{6,14},{7,15},{8,0},{9,1},... | collective-permute-start | bytes 589832 | tf_op jit(solution)/shard_map/ppermute | solution.py:26
  83.2 10.1 %collective-permute-start.30 = (bf16[2,384,128]{2,1,0:T(8,128)(2,1)S(1)}, bf16[2,384,128]{2,1,0:T(8,128)(2,1)S(1)}, u32[]{:S(2)}, u32[]{:S(2)}) collective-permute-start(bf16[2,384,128]{2,1,0:T(8,128)(2,1)S(1)} %get-tuple-element.71), channel_id=1, source_target_pairs={{0,8},{1,9},{2,10},{3,11},{4,12},{5,13},{6,14},{7,15},{8,0},{9,1},... | collective-permute-start | bytes 589832 | tf_op jit(solution)/shard_map/ppermute | solution.py:26
  84.4 9.0 %collective-permute-start.39 = (bf16[2,384,128]{2,1,0:T(8,128)(2,1)S(1)}, bf16[2,384,128]{2,1,0:T(8,128)(2,1)S(1)}, u32[]{:S(2)}, u32[]{:S(2)}) collective-permute-start(bf16[2,384,128]{2,1,0:T(8,128)(2,1)S(1)} %get-tuple-element.72), channel_id=1, source_target_pairs={{0,16},{1,17},{2,18},{3,19},{4,20},{5,21},{6,22},{7,23},{8,24},{9,... | collective-permute-start | bytes 589832 | tf_op jit(solution)/shard_map/ppermute | solution.py:26
  85.9 10.5 %collective-permute-start.36 = (bf16[2,384,128]{2,1,0:T(8,128)(2,1)S(1)}, bf16[2,384,128]{2,1,0:T(8,128)(2,1)S(1)}, u32[]{:S(2)}, u32[]{:S(2)}) collective-permute-start(bf16[2,384,128]{2,1,0:T(8,128)(2,1)S(1)} %get-tuple-element.76), channel_id=1, source_target_pairs={{0,16},{1,17},{2,18},{3,19},{4,20},{5,21},{6,22},{7,23},{8,24},{9,... | collective-permute-start | bytes 589832 | tf_op jit(solution)/shard_map/ppermute | solution.py:26
  90.0 8.2 %collective-permute-start.34 = (bf16[1,384,128]{2,1,0:T(8,128)(2,1)S(1)}, bf16[1,384,128]{2,1,0:T(8,128)(2,1)S(1)}, u32[]{:S(2)}, u32[]{:S(2)}) collective-permute-start(bf16[1,384,128]{2,1,0:T(8,128)(2,1)S(1)} %add_convert_fusion.33), channel_id=1, source_target_pairs={{0,16},{1,17},{2,18},{3,19},{4,20},{5,21},{6,22},{7,23},{8,24},{9,... | collective-permute-start | bytes 294920 | tf_op jit(solution)/shard_map/ppermute | solution.py:26
  93.4 11.3 %collective-permute-start.31 = (bf16[1,384,128]{2,1,0:T(8,128)(2,1)S(1)}, bf16[1,384,128]{2,1,0:T(8,128)(2,1)S(1)}, u32[]{:S(2)}, u32[]{:S(2)}) collective-permute-start(bf16[1,384,128]{2,1,0:T(8,128)(2,1)S(1)} %get-tuple-element.69), channel_id=1, source_target_pairs={{0,16},{1,17},{2,18},{3,19},{4,20},{5,21},{6,22},{7,23},{8,24},{9,... | collective-permute-start | bytes 294920 | tf_op jit(solution)/shard_map/ppermute | solution.py:26
  101.8 7.7 %collective-permute-start.35 = (bf16[1,384,128]{2,1,0:T(8,128)(2,1)S(1)}, bf16[1,384,128]{2,1,0:T(8,128)(2,1)S(1)}, u32[]{:S(2)}, u32[]{:S(2)}) collective-permute-start(bf16[1,384,128]{2,1,0:T(8,128)(2,1)S(1)} %get-tuple-element.73), channel_id=1, source_target_pairs={{0,4},{1,5},{2,6},{3,7},{4,0},{5,1},{6,2},{7,3},{8,12},{9,13},{10,... | collective-permute-start | bytes 294920 | tf_op jit(solution)/shard_map/ppermute | solution.py:42
  113.3 7.7 %collective-permute-start.45 = (bf16[384,128]{1,0:T(8,128)(2,1)S(1)}, bf16[384,128]{1,0:T(8,128)(2,1)S(1)}, u32[]{:S(2)}, u32[]{:S(2)}) collective-permute-start(bf16[384,128]{1,0:T(8,128)(2,1)S(1)} %fusion.1.refs_1_.refs_0_), channel_id=1, source_target_pairs={{0,4},{1,5},{2,6},{3,7},{4,0},{5,1},{6,2},{7,3},{8,12},{9,13},{10,... | collective-permute-start | bytes 294920 | tf_op jit(solution)/shard_map/ppermute | solution.py:42
  114.3 8.2 %collective-permute-start.42 = (bf16[384,128]{1,0:T(8,128)(2,1)S(1)}, bf16[384,128]{1,0:T(8,128)(2,1)S(1)}, u32[]{:S(2)}, u32[]{:S(2)}) collective-permute-start(bf16[384,128]{1,0:T(8,128)(2,1)S(1)} %fusion.1.refs_1_.refs_0_), channel_id=1, source_target_pairs={{0,1},{1,0},{2,3},{3,2},{4,5},{5,4},{6,7},{7,6},{8,9},{9,8},{10,11... | collective-permute-start | bytes 294920 | tf_op jit(solution)/shard_map/ppermute | solution.py:31
  115.2 8.2 %collective-permute-start.59 = (bf16[384,128]{1,0:T(8,128)(2,1)S(1)}, bf16[384,128]{1,0:T(8,128)(2,1)S(1)}, u32[]{:S(2)}, u32[]{:S(2)}) collective-permute-start(bf16[384,128]{1,0:T(8,128)(2,1)S(1)} %collective-permute-done.57.refs_16_), channel_id=1, source_target_pairs={{0,8},{1,9},{2,10},{3,11},{4,12},{5,13},{6,14},{7,15},{8,0},{9,1},... | collective-permute-start | bytes 294920 | tf_op jit(solution)/shard_map/ppermute | solution.py:26
  137.5 7.6 %collective-permute-start.52 = (bf16[384,128]{1,0:T(8,128)(2,1)S(1)}, bf16[384,128]{1,0:T(8,128)(2,1)S(1)}, u32[]{:S(2)}, u32[]{:S(2)}) collective-permute-start(bf16[384,128]{1,0:T(8,128)(2,1)S(1)} %collective-permute-done.51.refs_10_), channel_id=1, source_target_pairs={{0,1},{1,0},{2,3},{3,2},{4,5},{5,4},{6,7},{7,6},{8,9},{9,8},{10,11... | collective-permute-start | bytes 294920 | tf_op jit(solution)/shard_map/ppermute | solution.py:31
  154.8 7.8 %collective-permute-start.77 = (bf16[2,384,128]{2,1,0:T(8,128)(2,1)S(1)}, bf16[2,384,128]{2,1,0:T(8,128)(2,1)S(1)}, u32[]{:S(2)}, u32[]{:S(2)}) collective-permute-start(bf16[2,384,128]{2,1,0:T(8,128)(2,1)S(1)} %get-tuple-element.67), channel_id=1, source_target_pairs={{0,8},{1,9},{2,10},{3,11},{4,12},{5,13},{6,14},{7,15},{8,0},{9,1},... | collective-permute-start | bytes 589832 | tf_op jit(solution)/shard_map/ppermute | solution.py:26
  156.6 9.6 %collective-permute-start.74 = (bf16[2,384,128]{2,1,0:T(8,128)(2,1)S(1)}, bf16[2,384,128]{2,1,0:T(8,128)(2,1)S(1)}, u32[]{:S(2)}, u32[]{:S(2)}) collective-permute-start(bf16[2,384,128]{2,1,0:T(8,128)(2,1)S(1)} %get-tuple-element.63), channel_id=1, source_target_pairs={{0,8},{1,9},{2,10},{3,11},{4,12},{5,13},{6,14},{7,15},{8,0},{9,1},... | collective-permute-start | bytes 589832 | tf_op jit(solution)/shard_map/ppermute | solution.py:26
  157.6 8.6 %collective-permute-start.83 = (bf16[2,384,128]{2,1,0:T(8,128)(2,1)S(1)}, bf16[2,384,128]{2,1,0:T(8,128)(2,1)S(1)}, u32[]{:S(2)}, u32[]{:S(2)}) collective-permute-start(bf16[2,384,128]{2,1,0:T(8,128)(2,1)S(1)} %get-tuple-element.64), channel_id=1, source_target_pairs={{0,16},{1,17},{2,18},{3,19},{4,20},{5,21},{6,22},{7,23},{8,24},{9,... | collective-permute-start | bytes 589832 | tf_op jit(solution)/shard_map/ppermute | solution.py:26
  158.7 10.8 %collective-permute-start.80 = (bf16[2,384,128]{2,1,0:T(8,128)(2,1)S(1)}, bf16[2,384,128]{2,1,0:T(8,128)(2,1)S(1)}, u32[]{:S(2)}, u32[]{:S(2)}) collective-permute-start(bf16[2,384,128]{2,1,0:T(8,128)(2,1)S(1)} %get-tuple-element.68), channel_id=1, source_target_pairs={{0,16},{1,17},{2,18},{3,19},{4,20},{5,21},{6,22},{7,23},{8,24},{9,... | collective-permute-start | bytes 589832 | tf_op jit(solution)/shard_map/ppermute | solution.py:26
  162.6 9.0 %collective-permute-start.78 = (bf16[1,384,128]{2,1,0:T(8,128)(2,1)S(1)}, bf16[1,384,128]{2,1,0:T(8,128)(2,1)S(1)}, u32[]{:S(2)}, u32[]{:S(2)}) collective-permute-start(bf16[1,384,128]{2,1,0:T(8,128)(2,1)S(1)} %add_convert_fusion.26), channel_id=1, source_target_pairs={{0,16},{1,17},{2,18},{3,19},{4,20},{5,21},{6,22},{7,23},{8,24},{9,... | collective-permute-start | bytes 294920 | tf_op jit(solution)/shard_map/ppermute | solution.py:26
  166.3 11.5 %collective-permute-start.75 = (bf16[1,384,128]{2,1,0:T(8,128)(2,1)S(1)}, bf16[1,384,128]{2,1,0:T(8,128)(2,1)S(1)}, u32[]{:S(2)}, u32[]{:S(2)}) collective-permute-start(bf16[1,384,128]{2,1,0:T(8,128)(2,1)S(1)} %get-tuple-element.61), channel_id=1, source_target_pairs={{0,16},{1,17},{2,18},{3,19},{4,20},{5,21},{6,22},{7,23},{8,24},{9,... | collective-permute-start | bytes 294920 | tf_op jit(solution)/shard_map/ppermute | solution.py:26
  173.0 8.8 %collective-permute-start.79 = (bf16[1,384,128]{2,1,0:T(8,128)(2,1)S(1)}, bf16[1,384,128]{2,1,0:T(8,128)(2,1)S(1)}, u32[]{:S(2)}, u32[]{:S(2)}) collective-permute-start(bf16[1,384,128]{2,1,0:T(8,128)(2,1)S(1)} %get-tuple-element.65), channel_id=1, source_target_pairs={{0,4},{1,5},{2,6},{3,7},{4,0},{5,1},{6,2},{7,3},{8,12},{9,13},{10,... | collective-permute-start | bytes 294920 | tf_op jit(solution)/shard_map/ppermute | solution.py:42
  186.8 8.3 %collective-permute-start.89 = (bf16[384,128]{1,0:T(8,128)(2,1)S(1)}, bf16[384,128]{1,0:T(8,128)(2,1)S(1)}, u32[]{:S(2)}, u32[]{:S(2)}) collective-permute-start(bf16[384,128]{1,0:T(8,128)(2,1)S(1)} %bitcast.13), channel_id=1, source_target_pairs={{0,4},{1,5},{2,6},{3,7},{4,0},{5,1},{6,2},{7,3},{8,12},{9,13},{10,... | collective-permute-start | bytes 294920 | tf_op jit(solution)/shard_map/ppermute | solution.py:42
  187.4 7.6 %collective-permute-start.87 = (bf16[384,128]{1,0:T(8,128)(2,1)S(1)}, bf16[384,128]{1,0:T(8,128)(2,1)S(1)}, u32[]{:S(2)}, u32[]{:S(2)}) collective-permute-start(bf16[384,128]{1,0:T(8,128)(2,1)S(1)} %bitcast.14), channel_id=1, source_target_pairs={{0,2},{1,3},{2,4},{3,5},{4,6},{5,7},{6,0},{7,1},{8,10},{9,11},{10,... | collective-permute-start | bytes 294920 | tf_op jit(solution)/shard_map/ppermute | solution.py:42
  187.4 8.7 %collective-permute-start.86 = (bf16[384,128]{1,0:T(8,128)(2,1)S(1)}, bf16[384,128]{1,0:T(8,128)(2,1)S(1)}, u32[]{:S(2)}, u32[]{:S(2)}) collective-permute-start(bf16[384,128]{1,0:T(8,128)(2,1)S(1)} %bitcast.15), channel_id=1, source_target_pairs={{0,1},{1,0},{2,3},{3,2},{4,5},{5,4},{6,7},{7,6},{8,9},{9,8},{10,11... | collective-permute-start | bytes 294920 | tf_op jit(solution)/shard_map/ppermute | solution.py:31
  187.7 8.7 %collective-permute-start.103 = (bf16[384,128]{1,0:T(8,128)(2,1)S(1)}, bf16[384,128]{1,0:T(8,128)(2,1)S(1)}, u32[]{:S(2)}, u32[]{:S(2)}) collective-permute-start(bf16[384,128]{1,0:T(8,128)(2,1)S(1)} %collective-permute-done.101.refs_17_), channel_id=1, source_target_pairs={{0,8},{1,9},{2,10},{3,11},{4,12},{5,13},{6,14},{7,15},{8,0},{9,1},... | collective-permute-start | bytes 294920 | tf_op jit(solution)/shard_map/ppermute | solution.py:26
  212.0 7.5 %collective-permute-start.96 = (bf16[384,128]{1,0:T(8,128)(2,1)S(1)}, bf16[384,128]{1,0:T(8,128)(2,1)S(1)}, u32[]{:S(2)}, u32[]{:S(2)}) collective-permute-start(bf16[384,128]{1,0:T(8,128)(2,1)S(1)} %collective-permute-done.95.refs_11_), channel_id=1, source_target_pairs={{0,1},{1,0},{2,3},{3,2},{4,5},{5,4},{6,7},{7,6},{8,9},{9,8},{10,11... | collective-permute-start | bytes 294920 | tf_op jit(solution)/shard_map/ppermute | solution.py:31
  231.9 7.8 %collective-permute-start.118 = (bf16[2,384,128]{2,1,0:T(8,128)(2,1)S(1)}, bf16[2,384,128]{2,1,0:T(8,128)(2,1)S(1)}, u32[]{:S(2)}, u32[]{:S(2)}) collective-permute-start(bf16[2,384,128]{2,1,0:T(8,128)(2,1)S(1)} %add_convert_fusion.1), channel_id=1, source_target_pairs={{0,8},{1,9},{2,10},{3,11},{4,12},{5,13},{6,14},{7,15},{8,0},{9,1},... | collective-permute-start | bytes 589832 | tf_op jit(solution)/shard_map/ppermute | solution.py:26
  232.5 10.9 %collective-permute-start.120 = (bf16[2,384,128]{2,1,0:T(8,128)(2,1)S(1)}, bf16[2,384,128]{2,1,0:T(8,128)(2,1)S(1)}, u32[]{:S(2)}, u32[]{:S(2)}) collective-permute-start(bf16[2,384,128]{2,1,0:T(8,128)(2,1)S(1)} %add_convert_fusion), channel_id=1, source_target_pairs={{0,8},{1,9},{2,10},{3,11},{4,12},{5,13},{6,14},{7,15},{8,0},{9,1},... | collective-permute-start | bytes 589832 | tf_op jit(solution)/shard_map/ppermute | solution.py:26
  254.2 9.6 %collective-permute-start.127 = (bf16[384,128]{1,0:T(8,128)(2,1)S(1)}, bf16[384,128]{1,0:T(8,128)(2,1)S(1)}, u32[]{:S(2)}, u32[]{:S(2)}) collective-permute-start(bf16[384,128]{1,0:T(8,128)(2,1)S(1)} %bitcast.20), channel_id=1, source_target_pairs={{0,4},{1,5},{2,6},{3,7},{4,0},{5,1},{6,2},{7,3},{8,12},{9,13},{10,... | collective-permute-start | bytes 294920 | tf_op jit(solution)/shard_map/ppermute | solution.py:42
  254.8 9.0 %collective-permute-start.125 = (bf16[384,128]{1,0:T(8,128)(2,1)S(1)}, bf16[384,128]{1,0:T(8,128)(2,1)S(1)}, u32[]{:S(2)}, u32[]{:S(2)}) collective-permute-start(bf16[384,128]{1,0:T(8,128)(2,1)S(1)} %bitcast.21), channel_id=1, source_target_pairs={{0,2},{1,3},{2,4},{3,5},{4,6},{5,7},{6,0},{7,1},{8,10},{9,11},{10,... | collective-permute-start | bytes 294920 | tf_op jit(solution)/shard_map/ppermute | solution.py:42
  254.8 10.7 %collective-permute-start.124 = (bf16[384,128]{1,0:T(8,128)(2,1)S(1)}, bf16[384,128]{1,0:T(8,128)(2,1)S(1)}, u32[]{:S(2)}, u32[]{:S(2)}) collective-permute-start(bf16[384,128]{1,0:T(8,128)(2,1)S(1)} %bitcast.22), channel_id=1, source_target_pairs={{0,1},{1,0},{2,3},{3,2},{4,5},{5,4},{6,7},{7,6},{8,9},{9,8},{10,11... | collective-permute-start | bytes 294920 | tf_op jit(solution)/shard_map/ppermute | solution.py:31
  255.4 10.5 %collective-permute-start.132 = (bf16[384,128]{1,0:T(8,128)(2,1)S(1)}, bf16[384,128]{1,0:T(8,128)(2,1)S(1)}, u32[]{:S(2)}, u32[]{:S(2)}) collective-permute-start(bf16[384,128]{1,0:T(8,128)(2,1)S(1)} %collective-permute-done.131.refs_9_), channel_id=1, source_target_pairs={{0,1},{1,0},{2,3},{3,2},{4,5},{5,4},{6,7},{7,6},{8,9},{9,8},{10,11... | collective-permute-start | bytes 294920 | tf_op jit(solution)/shard_map/ppermute | solution.py:31
  257.4 8.5 %collective-permute-start.137 = (bf16[384,128]{1,0:T(8,128)(2,1)S(1)}, bf16[384,128]{1,0:T(8,128)(2,1)S(1)}, u32[]{:S(2)}, u32[]{:S(2)}) collective-permute-start(bf16[384,128]{1,0:T(8,128)(2,1)S(1)} %collective-permute-done.129.refs_7_), channel_id=1, source_target_pairs={{0,8},{1,9},{2,10},{3,11},{4,12},{5,13},{6,14},{7,15},{8,0},{9,1},... | collective-permute-start | bytes 294920 | tf_op jit(solution)/shard_map/ppermute | solution.py:26
  265.9 7.7 %collective-permute-start.128 = (bf16[384,128]{1,0:T(8,128)(2,1)S(1)}, bf16[384,128]{1,0:T(8,128)(2,1)S(1)}, u32[]{:S(2)}, u32[]{:S(2)}) collective-permute-start(bf16[384,128]{1,0:T(8,128)(2,1)S(1)} %collective-permute-done.127.refs_5_), channel_id=1, source_target_pairs={{0,1},{1,0},{2,3},{3,2},{4,5},{5,4},{6,7},{7,6},{8,9},{9,8},{10,11... | collective-permute-start | bytes 294920 | tf_op jit(solution)/shard_map/ppermute | solution.py:31
  265.9 7.7 %collective-permute-start.126 = (bf16[384,128]{1,0:T(8,128)(2,1)S(1)}, bf16[384,128]{1,0:T(8,128)(2,1)S(1)}, u32[]{:S(2)}, u32[]{:S(2)}) collective-permute-start(bf16[384,128]{1,0:T(8,128)(2,1)S(1)} %collective-permute-done.125.refs_3_), channel_id=1, source_target_pairs={{0,1},{1,0},{2,3},{3,2},{4,5},{5,4},{6,7},{7,6},{8,9},{9,8},{10,11... | collective-permute-start | bytes 294920 | tf_op jit(solution)/shard_map/ppermute | solution.py:31
  280.8 7.6 %collective-permute-start.143 = (bf16[1,384,128]{2,1,0:T(8,128)(2,1)S(1)}, bf16[1,384,128]{2,1,0:T(8,128)(2,1)S(1)}, u32[]{:S(2)}, u32[]{:S(2)}) collective-permute-start(bf16[1,384,128]{2,1,0:T(8,128)(2,1)S(1)} %add_convert_fusion.13), channel_id=1, source_target_pairs={{0,2},{1,3},{2,4},{3,5},{4,6},{5,7},{6,0},{7,1},{8,10},{9,11},{10,... | collective-permute-start | bytes 294920 | tf_op jit(solution)/shard_map/ppermute | solution.py:42
  282.1 9.9 %collective-permute-start.141 = (bf16[1,384,128]{2,1,0:T(8,128)(2,1)S(1)}, bf16[1,384,128]{2,1,0:T(8,128)(2,1)S(1)}, u32[]{:S(2)}, u32[]{:S(2)}) collective-permute-start(bf16[1,384,128]{2,1,0:T(8,128)(2,1)S(1)} %get-tuple-element.81), channel_id=1, source_target_pairs={{0,4},{1,5},{2,6},{3,7},{4,0},{5,1},{6,2},{7,3},{8,12},{9,13},{10,... | collective-permute-start | bytes 294920 | tf_op jit(solution)/shard_map/ppermute | solution.py:42
  282.2 9.8 %collective-permute-start.142 = (bf16[1,384,128]{2,1,0:T(8,128)(2,1)S(1)}, bf16[1,384,128]{2,1,0:T(8,128)(2,1)S(1)}, u32[]{:S(2)}, u32[]{:S(2)}) collective-permute-start(bf16[1,384,128]{2,1,0:T(8,128)(2,1)S(1)} %get-tuple-element.82), channel_id=1, source_target_pairs={{0,6},{1,7},{2,0},{3,1},{4,2},{5,3},{6,4},{7,5},{8,14},{9,15},{10,... | collective-permute-start | bytes 294920 | tf_op jit(solution)/shard_map/ppermute | solution.py:42
  (99 other events, 577.1 us)
